TPU v7x, 32 devices: a whole 2x2x4 slice. The times are simulated.
32 devices in a mesh: dx: 2 (over x), dy: 16 (over z, y, core).
Axes of the slice: x: 2, y: 2, z: 4, core: 2. Of those that a mesh axis runs over, the one named last changes fastest.
Arguments:
- seg_mid: float32 [2, 16, 3, 4096], P('dx', 'dy'), may hold values from 0 to 1
- seg_line: float32 [2, 16, 3, 4096], P('dx', 'dy'), may hold values from -0.3 to 0.3
- seg_burgers: float32 [2, 16, 3, 4096], P('dx', 'dy'), may hold values from -5 to 5
- seg_cell: int32 [2, 16, 4096], P('dx', 'dy'), may hold values from 0 to 71, as said below
- seg_node: int32 [2, 16, 2, 4096], P('dx', 'dy'), may hold values from 0 to 4607, as said below
- ghost_list: int32 [2, 16, 8, 2], P('dx', 'dy'), may hold values from 0 to 31
- ghost_count: int32 [2, 16, 8], P('dx', 'dy'), may hold values from 1 to 2
- pair_list: int32 [2, 16, 32, 12], P('dx', 'dy'), may hold values from 0 to 47, as said below
- pair_count: int32 [2, 16, 32], P('dx', 'dy'), may hold values from 1 to 12
Outputs:
- node_force: float32 [2, 16, 3, 512], P('dx', 'dy')
- cell_moments: float32 [315, 256], P(None, ('dx', 'dy'))
Inputs may be any that keep to these rules, and one draw needn't show every extreme that they name: `seg_node`: each entry is d * 512 + m with m a node of the domain at offset (a, b) from the segment's domain, d = 3 (a + 1) + (b + 1), a and b in -1, 0, 1; d = 4 is the domain itself. `seg_cell`: each entry is d * 8 + c with c a cell owned by the domain at offset (a, b) from the segment's domain, d = 3 (a + 1) + (b + 1), a and b in -1, 0, 1; d = 4 is the domain itself. `pair_list`: the entries of one tile's list are distinct.
All inputs are finite; a program needn't handle non-finite values.
Results may differ from a plain program's by a relative error of at most 0.0003.
Values sent between devices are 32-bit elements; how exact they have to be, the bound alone decides.
No kernel may reach another device: no remote copies, remote signals or barrier semaphores. Data moves between devices by JAX's collectives and lax.ppermute only.
A program may use at most 64 MiB of HBM per device.

v0:
```python
import jax
import jax.numpy as jnp
import numpy as np
from jax import lax
from jax.sharding import PartitionSpec as P

TILE = 128
GHOST = 2
NP = 12
NODE_DEV = 512
CELL_DEV = 8


core_radius = 0.1
shear_scale = 0.25
highest = lax.Precision.HIGHEST
neighbour_offsets = ((-1, -1), (-1, 0), (-1, 1), (0, -1), (0, 1), (1, -1), (1, 0), (1, 1))


def passed_along(block, axis, distance):
    devices = range(lax.axis_size(axis))
    route = [((i - distance) % len(devices), i) for i in devices]
    return lax.ppermute(block, axis, route)


def exponent_table():
    exponent_rows = []
    for degree in range(5):
        for first_power in range(degree, -1, -1):
            for second in range(degree - first_power, -1, -1):
                exponent_rows.append((first_power, second, degree - first_power - second))
    return np.array(exponent_rows, dtype=np.int32)


def moment_terms(midpoint, line_vector, burgers):
    scaled = 2.0 * (midpoint - 0.5)
    powers = jnp.stack(
        [jnp.ones_like(scaled), scaled, scaled * scaled, scaled**3, scaled**4], axis=1
    )
    exponents = exponent_table()
    monomial = powers[0, exponents[:, 0]] * powers[1, exponents[:, 1]] * powers[2, exponents[:, 2]]
    products = (burgers[:, None, :] * line_vector[None, :, :]).reshape(9, -1)
    return (products[:, None, :] * monomial[None, :, :]).reshape(9 * monomial.shape[0], -1)


def pair_stress(field_tiles, source_tiles, valid_weight):
    separation = [
        field_tiles[component][:, :, None] - source_tiles[component][:, None, :]
        for component in range(3)
    ]
    line_source = source_tiles[3:6]
    burgers_source = source_tiles[6:9]
    cross_source = [
        burgers_source[1] * line_source[2] - burgers_source[2] * line_source[1],
        burgers_source[2] * line_source[0] - burgers_source[0] * line_source[2],
        burgers_source[0] * line_source[1] - burgers_source[1] * line_source[0],
    ]
    cross_source = [entry_value[:, None, :] for entry_value in cross_source]
    radius_sq = separation[0] ** 2 + separation[1] ** 2 + separation[2] ** 2 + core_radius**2
    inverse = 1.0 / jnp.sqrt(radius_sq)
    weight = shear_scale * valid_weight[:, None, None] * inverse / radius_sq
    projection = (
        separation[0] * cross_source[0]
        + separation[1] * cross_source[1]
        + separation[2] * cross_source[2]
    )
    diagonal_term = projection * (1.0 + 1.5 * core_radius**2 / radius_sq)
    entries = []
    for first_axis, second_axis in ((0, 0), (1, 1), (2, 2), (0, 1), (0, 2), (1, 2)):
        entry_value = (
            separation[first_axis] * cross_source[second_axis]
            + separation[second_axis] * cross_source[first_axis]
            - 3.0 * projection * separation[first_axis] * separation[second_axis] / radius_sq
        )
        if first_axis == second_axis:
            entry_value = entry_value + diagonal_term
        entries.append(jnp.sum(weight * entry_value, axis=2))
    return jnp.stack(entries)


def segment_force(stress, own_columns):
    line_vector = own_columns[3:6]
    burgers = own_columns[6:9]
    traction = [
        stress[0] * burgers[0] + stress[3] * burgers[1] + stress[4] * burgers[2],
        stress[3] * burgers[0] + stress[1] * burgers[1] + stress[5] * burgers[2],
        stress[4] * burgers[0] + stress[5] * burgers[1] + stress[2] * burgers[2],
    ]
    return jnp.stack(
        [
            traction[1] * line_vector[2] - traction[2] * line_vector[1],
            traction[2] * line_vector[0] - traction[0] * line_vector[2],
            traction[0] * line_vector[1] - traction[1] * line_vector[0],
        ]
    )


def on_device(
    seg_mid,
    seg_line,
    seg_burgers,
    seg_cell,
    seg_node,
    ghost_list,
    ghost_count,
    pair_list,
    pair_count,
):
    seg_data = jnp.concatenate([seg_mid[0, 0], seg_line[0, 0], seg_burgers[0, 0]], axis=0)
    own_count = seg_data.shape[1] // TILE
    own_tiles = seg_data.reshape(9, own_count, TILE).transpose(1, 0, 2)
    packets = own_tiles[ghost_list[0, 0]]
    slot_valid = (jnp.arange(GHOST, dtype=jnp.int32)[None, :] < ghost_count[0, 0][:, None]).astype(
        jnp.float32
    )
    packets = packets * slot_valid[:, :, None, None]
    along_x = [
        passed_along(outgoing, "dx", stride)
        for stride, outgoing in ((1, packets[5:8]), (-1, packets[0:3]))
    ]
    from_left = along_x[0]
    from_right = along_x[1]
    upward = jnp.stack([packets[4], from_left[2], from_right[2]])
    downward = jnp.stack([packets[3], from_left[0], from_right[0]])
    along_y = [
        passed_along(outgoing, "dy", stride) for stride, outgoing in ((1, upward), (-1, downward))
    ]
    from_below = along_y[0]
    from_above = along_y[1]
    terms = moment_terms(seg_mid[0, 0], seg_line[0, 0], seg_burgers[0, 0])
    cell_columns = jnp.arange(9 * CELL_DEV, dtype=jnp.int32)
    membership = (seg_cell[0, 0][:, None] == cell_columns[None, :]).astype(jnp.float32)
    moment_partial = jnp.dot(
        terms, membership, precision=highest, preferred_element_type=jnp.float32
    )
    cell_grid = moment_partial.reshape(moment_partial.shape[0], 3, 3, CELL_DEV)
    cell_rows = [
        passed_along(cell_grid[:, :, column], "dy", stride) for stride, column in ((1, 2), (-1, 0))
    ]
    cell_middle = cell_grid[:, :, 1] + cell_rows[0] + cell_rows[1]
    cell_cols = [
        passed_along(cell_middle[:, column], "dx", stride) for stride, column in ((1, 2), (-1, 0))
    ]
    cell_moments = cell_middle[:, 1] + cell_cols[0] + cell_cols[1]
    groups = [
        from_below[1],
        from_left[1],
        from_above[1],
        from_below[0],
        from_above[0],
        from_below[2],
        from_right[1],
        from_above[2],
    ]
    shifted = []
    for group_index in range(8):
        first_shift, second_shift = neighbour_offsets[group_index]
        offset_rows = jnp.array([first_shift, second_shift, 0, 0, 0, 0, 0, 0, 0], jnp.float32)
        shifted.append(groups[group_index] + offset_rows[None, :, None])
    source_pool = jnp.concatenate([own_tiles] + shifted, axis=0)
    own_columns = own_tiles.transpose(1, 0, 2)
    pair_rows = pair_list[0, 0]
    pair_limit = pair_count[0, 0]

    def add_slot(stress_total, slot_index):
        source_tiles = source_pool[pair_rows[:, slot_index]].transpose(1, 0, 2)
        valid_weight = (slot_index < pair_limit).astype(jnp.float32)
        return (stress_total + pair_stress(own_columns, source_tiles, valid_weight), None)

    stress_total, unused = lax.scan(
        add_slot, jnp.zeros((6, own_count, TILE), jnp.float32), jnp.arange(NP, dtype=jnp.int32)
    )
    force = segment_force(stress_total, own_columns).reshape(3, own_count * TILE)
    node_columns = jnp.arange(9 * NODE_DEV, dtype=jnp.int32)
    node_ends = seg_node[0, 0]
    incidence = (node_ends[0][:, None] == node_columns[None, :]).astype(jnp.float32) + (
        node_ends[1][:, None] == node_columns[None, :]
    ).astype(jnp.float32)
    node_partial = jnp.dot(
        0.5 * force, incidence, precision=highest, preferred_element_type=jnp.float32
    )
    node_grid = node_partial.reshape(3, 3, 3, NODE_DEV)
    along_rows = [
        passed_along(node_grid[:, row], "dx", stride) for stride, row in ((1, 2), (-1, 0))
    ]
    partial_mid = node_grid[:, 1] + along_rows[0] + along_rows[1]
    along_cols = [
        passed_along(partial_mid[:, column], "dy", stride) for stride, column in ((1, 2), (-1, 0))
    ]
    node_total = partial_mid[:, 1] + along_cols[0] + along_cols[1]
    return (node_total[None, None], cell_moments)


def solution(mesh):
    in_specs = (
        P("dx", "dy", None, None),
        P("dx", "dy", None, None),
        P("dx", "dy", None, None),
        P("dx", "dy", None),
        P("dx", "dy", None, None),
        P("dx", "dy", None, None),
        P("dx", "dy", None),
        P("dx", "dy", None, None),
        P("dx", "dy", None),
    )
    out_specs = (P("dx", "dy", None, None), P(None, ("dx", "dy")))
    return jax.shard_map(
        on_device, mesh=mesh, in_specs=in_specs, out_specs=out_specs, check_vma=False
    )
```

profile of v0, /device:TPU:0, one launch (start us, length us, event | category | flops | bytes accessed | tf_op | source)
XLA Modules:
  0.0 264.8 jit_solution(2471241427780326510)
XLA Ops:
  3.9 3.0 %collective-permute-start = (f32[3,2,9,128]{3,2,1,0:T(8,128)S(1)}, f32[3,2,9,128]{3,2,1,0:T(8,128)S(1)}, u32[]{:S(2)}, u32[]{:S(2)}) collective-permute-start(f32[3,2,9,128]{3,2,1,0:T(8,128)S(1)} %get-tuple-element.106), channel_id=1, source_target_pairs={{16,0},{0,16},{17,1},{1,17},{18,2},{2,18},{19,3},{3,19},{20,4},{4,... | collective-permute-start | bytes 82952 | tf_op jit(solution)/shard_map/ppermute | solution.py:23
  10.6 2.0 gather_fusion.2
  12.7 2.0 gather_fusion.3
  14.7 2.0 gather_fusion.4
  17.0 3.3 %broadcast_multiply_fusion = f32[9,35,4096]{2,1,0:T(8,128)} fusion(f32[35,4096]{1,0:T(8,128)S(1)} %multiply_multiply_fusion, f32[9,4096]{1,0:T(8,128)S(1)} %mul.423), kind=kLoop, calls=%fused_computation.95 | loop fusion | flops 1290240 | bytes 5881856 | tf_op jit(solution)/shard_map/mul | solution.py:43
  20.2 7.3 %reshape.357 = f32[315,4096,1,1]{1,0,2,3:T(8,128)} reshape(f32[9,35,4096]{2,1,0:T(8,128)} %broadcast_multiply_fusion) | data formatting | bytes 10321920 | tf_op jit(solution)/shard_map/mul | solution.py:43
  27.6 5.3 %fusion.50 = f32[315,3,3,8]{0,3,2,1:T(8,128)S(1)} fusion(f32[315,4096,1,1]{1,0,2,3:T(8,128)} %reshape.357, s32[3,3,8]{2,1,0:T(4,128)S(1)} %multiply_add_fusion.4, s32[4096]{0:T(1024)S(1)} %bitcast.234), kind=kOutput, calls=%fused_computation.93 | convolution fusion | flops 1115062272 | bytes 5268352 | tf_op jit(solution)/shard_map/dot_general | solution.py:133
  33.0 4.4 %collective-permute-start.9 = (f32[315,3,8]{0,2,1:T(8,128)S(1)}, f32[315,3,8]{0,2,1:T(8,128)S(1)}, u32[]{:S(2)}, u32[]{:S(2)}) collective-permute-start(f32[315,3,8]{0,2,1:T(8,128)S(1)} %get-tuple-element.109), channel_id=1, source_target_pairs={{1,0},{2,1},{3,2},{4,3},{5,4},{6,5},{7,6},{8,7},{9,8},{10,9},{11,1... | collective-permute-start | bytes 90728 | tf_op jit(solution)/shard_map/ppermute | solution.py:23
  37.8 4.4 %collective-permute-start.3 = (f32[3,2,9,128]{3,2,1,0:T(8,128)S(1)}, f32[3,2,9,128]{3,2,1,0:T(8,128)S(1)}, u32[]{:S(2)}, u32[]{:S(2)}) collective-permute-start(f32[3,2,9,128]{3,2,1,0:T(8,128)S(1)} %pad_maximum_fusion.2), channel_id=1, source_target_pairs={{1,0},{2,1},{3,2},{4,3},{5,4},{6,5},{7,6},{8,7},{9,8},{10,9},{11,1... | collective-permute-start | bytes 82952 | tf_op jit(solution)/shard_map/ppermute | solution.py:23
  44.6 139.4 %while.11 = (s32[]{:T(128)}, f32[6,32,128]{2,1,0:T(8,128)S(1)}, f32[9,32,128]{2,1,0:T(8,128)S(1)}, s32[12]{0:T(128)S(1)}, s32[32,12]{0,1:T(8,128)S(1)}, /*index=...) while((s32[]{:T(128)}, f32[6,32,128]{2,1,0:T(8,128)S(1)}, ...), condition=%wide.region_7.8_spmd.clone, body=%wide.region_0.7_spmd.clone.sunk | while | flops 35714212 | bytes 1381413 | solution.py:170
  48.6 7.5 %fusion.99 = (f32[32,128]{1,0:T(8,128)S(1)}, f32[32,128]{1,0:T(8,128)S(1)}, f32[32,128]{1,0:T(8,128)S(1)}, f32[32,128]{1,0:T(8,128)S(1)}, f32[32,128]{1,0:T(8,128)S(1)}, /*index=5*/f32[32,128]{1,0:T(8,128)S(1)}) fusion(f32[32,128]{1,0:T(8,128)S(1)} %bitcast.211, f32[32,128]{1,0:T(8,128)S(1)} %bitcast.210, f32[32,128]{1,0:T(8,128)S(1)} %bitcast.212, ...), kind=kLoop, calls=%fused_computation.62.clone.1 | loop fusion | flops 35627008 | bytes 245888 | tf_op jit(solution)/shard_map/while/body/eval_jaxpr/reduce_sum | solution.py:77
  60.2 7.5 %fusion.99 = (f32[32,128]{1,0:T(8,128)S(1)}, f32[32,128]{1,0:T(8,128)S(1)}, f32[32,128]{1,0:T(8,128)S(1)}, f32[32,128]{1,0:T(8,128)S(1)}, f32[32,128]{1,0:T(8,128)S(1)}, /*index=5*/f32[32,128]{1,0:T(8,128)S(1)}) fusion(f32[32,128]{1,0:T(8,128)S(1)} %bitcast.211, f32[32,128]{1,0:T(8,128)S(1)} %bitcast.210, f32[32,128]{1,0:T(8,128)S(1)} %bitcast.212, ...), kind=kLoop, calls=%fused_computation.62.clone.1 | loop fusion | flops 35627008 | bytes 245888 | tf_op jit(solution)/shard_map/while/body/eval_jaxpr/reduce_sum | solution.py:77
  71.8 7.5 %fusion.99 = (f32[32,128]{1,0:T(8,128)S(1)}, f32[32,128]{1,0:T(8,128)S(1)}, f32[32,128]{1,0:T(8,128)S(1)}, f32[32,128]{1,0:T(8,128)S(1)}, f32[32,128]{1,0:T(8,128)S(1)}, /*index=5*/f32[32,128]{1,0:T(8,128)S(1)}) fusion(f32[32,128]{1,0:T(8,128)S(1)} %bitcast.211, f32[32,128]{1,0:T(8,128)S(1)} %bitcast.210, f32[32,128]{1,0:T(8,128)S(1)} %bitcast.212, ...), kind=kLoop, calls=%fused_computation.62.clone.1 | loop fusion | flops 35627008 | bytes 245888 | tf_op jit(solution)/shard_map/while/body/eval_jaxpr/reduce_sum | solution.py:77
  83.4 7.5 %fusion.99 = (f32[32,128]{1,0:T(8,128)S(1)}, f32[32,128]{1,0:T(8,128)S(1)}, f32[32,128]{1,0:T(8,128)S(1)}, f32[32,128]{1,0:T(8,128)S(1)}, f32[32,128]{1,0:T(8,128)S(1)}, /*index=5*/f32[32,128]{1,0:T(8,128)S(1)}) fusion(f32[32,128]{1,0:T(8,128)S(1)} %bitcast.211, f32[32,128]{1,0:T(8,128)S(1)} %bitcast.210, f32[32,128]{1,0:T(8,128)S(1)} %bitcast.212, ...), kind=kLoop, calls=%fused_computation.62.clone.1 | loop fusion | flops 35627008 | bytes 245888 | tf_op jit(solution)/shard_map/while/body/eval_jaxpr/reduce_sum | solution.py:77
  95.0 7.5 %fusion.99 = (f32[32,128]{1,0:T(8,128)S(1)}, f32[32,128]{1,0:T(8,128)S(1)}, f32[32,128]{1,0:T(8,128)S(1)}, f32[32,128]{1,0:T(8,128)S(1)}, f32[32,128]{1,0:T(8,128)S(1)}, /*index=5*/f32[32,128]{1,0:T(8,128)S(1)}) fusion(f32[32,128]{1,0:T(8,128)S(1)} %bitcast.211, f32[32,128]{1,0:T(8,128)S(1)} %bitcast.210, f32[32,128]{1,0:T(8,128)S(1)} %bitcast.212, ...), kind=kLoop, calls=%fused_computation.62.clone.1 | loop fusion | flops 35627008 | bytes 245888 | tf_op jit(solution)/shard_map/while/body/eval_jaxpr/reduce_sum | solution.py:77
  106.7 7.5 %fusion.99 = (f32[32,128]{1,0:T(8,128)S(1)}, f32[32,128]{1,0:T(8,128)S(1)}, f32[32,128]{1,0:T(8,128)S(1)}, f32[32,128]{1,0:T(8,128)S(1)}, f32[32,128]{1,0:T(8,128)S(1)}, /*index=5*/f32[32,128]{1,0:T(8,128)S(1)}) fusion(f32[32,128]{1,0:T(8,128)S(1)} %bitcast.211, f32[32,128]{1,0:T(8,128)S(1)} %bitcast.210, f32[32,128]{1,0:T(8,128)S(1)} %bitcast.212, ...), kind=kLoop, calls=%fused_computation.62.clone.1 | loop fusion | flops 35627008 | bytes 245888 | tf_op jit(solution)/shard_map/while/body/eval_jaxpr/reduce_sum | solution.py:77
  118.3 7.5 %fusion.99 = (f32[32,128]{1,0:T(8,128)S(1)}, f32[32,128]{1,0:T(8,128)S(1)}, f32[32,128]{1,0:T(8,128)S(1)}, f32[32,128]{1,0:T(8,128)S(1)}, f32[32,128]{1,0:T(8,128)S(1)}, /*index=5*/f32[32,128]{1,0:T(8,128)S(1)}) fusion(f32[32,128]{1,0:T(8,128)S(1)} %bitcast.211, f32[32,128]{1,0:T(8,128)S(1)} %bitcast.210, f32[32,128]{1,0:T(8,128)S(1)} %bitcast.212, ...), kind=kLoop, calls=%fused_computation.62.clone.1 | loop fusion | flops 35627008 | bytes 245888 | tf_op jit(solution)/shard_map/while/body/eval_jaxpr/reduce_sum | solution.py:77
  129.9 7.5 %fusion.99 = (f32[32,128]{1,0:T(8,128)S(1)}, f32[32,128]{1,0:T(8,128)S(1)}, f32[32,128]{1,0:T(8,128)S(1)}, f32[32,128]{1,0:T(8,128)S(1)}, f32[32,128]{1,0:T(8,128)S(1)}, /*index=5*/f32[32,128]{1,0:T(8,128)S(1)}) fusion(f32[32,128]{1,0:T(8,128)S(1)} %bitcast.211, f32[32,128]{1,0:T(8,128)S(1)} %bitcast.210, f32[32,128]{1,0:T(8,128)S(1)} %bitcast.212, ...), kind=kLoop, calls=%fused_computation.62.clone.1 | loop fusion | flops 35627008 | bytes 245888 | tf_op jit(solution)/shard_map/while/body/eval_jaxpr/reduce_sum | solution.py:77
  141.5 7.5 %fusion.99 = (f32[32,128]{1,0:T(8,128)S(1)}, f32[32,128]{1,0:T(8,128)S(1)}, f32[32,128]{1,0:T(8,128)S(1)}, f32[32,128]{1,0:T(8,128)S(1)}, f32[32,128]{1,0:T(8,128)S(1)}, /*index=5*/f32[32,128]{1,0:T(8,128)S(1)}) fusion(f32[32,128]{1,0:T(8,128)S(1)} %bitcast.211, f32[32,128]{1,0:T(8,128)S(1)} %bitcast.210, f32[32,128]{1,0:T(8,128)S(1)} %bitcast.212, ...), kind=kLoop, calls=%fused_computation.62.clone.1 | loop fusion | flops 35627008 | bytes 245888 | tf_op jit(solution)/shard_map/while/body/eval_jaxpr/reduce_sum | solution.py:77
  153.1 7.5 %fusion.99 = (f32[32,128]{1,0:T(8,128)S(1)}, f32[32,128]{1,0:T(8,128)S(1)}, f32[32,128]{1,0:T(8,128)S(1)}, f32[32,128]{1,0:T(8,128)S(1)}, f32[32,128]{1,0:T(8,128)S(1)}, /*index=5*/f32[32,128]{1,0:T(8,128)S(1)}) fusion(f32[32,128]{1,0:T(8,128)S(1)} %bitcast.211, f32[32,128]{1,0:T(8,128)S(1)} %bitcast.210, f32[32,128]{1,0:T(8,128)S(1)} %bitcast.212, ...), kind=kLoop, calls=%fused_computation.62.clone.1 | loop fusion | flops 35627008 | bytes 245888 | tf_op jit(solution)/shard_map/while/body/eval_jaxpr/reduce_sum | solution.py:77
  164.7 7.5 %fusion.99 = (f32[32,128]{1,0:T(8,128)S(1)}, f32[32,128]{1,0:T(8,128)S(1)}, f32[32,128]{1,0:T(8,128)S(1)}, f32[32,128]{1,0:T(8,128)S(1)}, f32[32,128]{1,0:T(8,128)S(1)}, /*index=5*/f32[32,128]{1,0:T(8,128)S(1)}) fusion(f32[32,128]{1,0:T(8,128)S(1)} %bitcast.211, f32[32,128]{1,0:T(8,128)S(1)} %bitcast.210, f32[32,128]{1,0:T(8,128)S(1)} %bitcast.212, ...), kind=kLoop, calls=%fused_computation.62.clone.1 | loop fusion | flops 35627008 | bytes 245888 | tf_op jit(solution)/shard_map/while/body/eval_jaxpr/reduce_sum | solution.py:77
  176.4 7.5 %fusion.99 = (f32[32,128]{1,0:T(8,128)S(1)}, f32[32,128]{1,0:T(8,128)S(1)}, f32[32,128]{1,0:T(8,128)S(1)}, f32[32,128]{1,0:T(8,128)S(1)}, f32[32,128]{1,0:T(8,128)S(1)}, /*index=5*/f32[32,128]{1,0:T(8,128)S(1)}) fusion(f32[32,128]{1,0:T(8,128)S(1)} %bitcast.211, f32[32,128]{1,0:T(8,128)S(1)} %bitcast.210, f32[32,128]{1,0:T(8,128)S(1)} %bitcast.212, ...), kind=kLoop, calls=%fused_computation.62.clone.1 | loop fusion | flops 35627008 | bytes 245888 | tf_op jit(solution)/shard_map/while/body/eval_jaxpr/reduce_sum | solution.py:77
  184.1 68.3 %fusion.41 = f32[3,3,3,512]{3,0,2,1:T(4,128)S(1)} fusion(s32[4096]{0:T(1024)S(1)} %bitcast.229, s32[3,3,512]{2,1,0:T(4,128)S(1)} %multiply_add_fusion, s32[4096]{0:T(1024)S(1)} %bitcast.228, f32[1,4096]{1,0:T(1,128)S(1)} %bitcast.227, f32[1,4096]{1,0:T(1,128)S(1)} %bitcast.231, f32[1,4096]{1,0:T(1,128)S(1)} %bitcast.230), kind=kOutput, calls=%fused_computation.84 | convolution fusion | flops 773885952 | bytes 155648 | tf_op jit(solution)/shard_map/dot_general | solution.py:179
  258.4 4.4 %collective-permute-start.7 = (f32[3,512]{1,0:T(4,128)S(1)}, f32[3,512]{1,0:T(4,128)S(1)}, u32[]{:S(2)}, u32[]{:S(2)}) collective-permute-start(f32[3,512]{1,0:T(4,128)S(1)} %get-tuple-element.127), channel_id=1, source_target_pairs={{1,0},{2,1},{3,2},{4,3},{5,4},{6,5},{7,6},{8,7},{9,8},{10,9},{11,1... | collective-permute-start | bytes 18440 | tf_op jit(solution)/shard_map/ppermute | solution.py:23
  (277 shorter events, 41.8 us)
Async XLA Ops:
  3.9 33.8 %collective-permute-start = (f32[3,2,9,128]{3,2,1,0:T(8,128)S(1)}, f32[3,2,9,128]{3,2,1,0:T(8,128)S(1)}, u32[]{:S(2)}, u32[]{:S(2)}) collective-permute-start(f32[3,2,9,128]{3,2,1,0:T(8,128)S(1)} %get-tuple-element.106), channel_id=1, source_target_pairs={{16,0},{0,16},{17,1},{1,17},{18,2},{2,18},{19,3},{3,19},{20,4},{4,... | collective-permute-start | bytes 82952 | tf_op jit(solution)/shard_map/ppermute | solution.py:23
  6.9 30.8 %collective-permute-start.1 = (f32[3,2,9,128]{3,2,1,0:T(8,128)S(1)}, f32[3,2,9,128]{3,2,1,0:T(8,128)S(1)}, u32[]{:S(2)}, u32[]{:S(2)}) collective-permute-start(f32[3,2,9,128]{3,2,1,0:T(8,128)S(1)} %get-tuple-element.107), channel_id=1, source_target_pairs={{16,0},{0,16},{17,1},{1,17},{18,2},{2,18},{19,3},{3,19},{20,4},{4,... | collective-permute-start | bytes 82952 | tf_op jit(solution)/shard_map/ppermute | solution.py:23
  27.5 10.1 %copy-start.5 = (f32[1,1,3,4096]{3,1,2,0:T(1,128)S(1)}, f32[1,1,3,4096]{3,1,2,0:T(1,128)}, u32[]{:S(2)}) copy-start(f32[1,1,3,4096]{3,1,2,0:T(1,128)} %param.26) | copy-start | bytes 147460
  27.5 10.1 %copy-start.6 = (s32[1,1,2,4096]{3,2,1,0:T(2,128)S(1)}, s32[1,1,2,4096]{3,2,1,0:T(2,128)}, u32[]{:S(2)}) copy-start(s32[1,1,2,4096]{3,2,1,0:T(2,128)} %param.29) | copy-start | bytes 98308
  27.5 10.2 %copy-start.7 = (s32[1,1,32,12]{2,1,3,0:T(1,128)S(1)}, s32[1,1,32,12]{2,1,3,0:T(1,128)}, u32[]{:S(2)}) copy-start(s32[1,1,32,12]{2,1,3,0:T(1,128)} %param.32) | copy-start | bytes 4612
  27.5 16.5 %copy-start.15 = (f32[9]{0:T(128)S(1)}, f32[9]{0:T(128)}, u32[]{:S(2)}) copy-start(f32[9]{0:T(128)} %constant.84.clone) | copy-start | bytes 112
  27.5 16.6 %copy-start.14 = (f32[9]{0:T(128)S(1)}, f32[9]{0:T(128)}, u32[]{:S(2)}) copy-start(f32[9]{0:T(128)} %constant.85.clone) | copy-start | bytes 112
  27.6 16.6 %copy-start.13 = (f32[9]{0:T(128)S(1)}, f32[9]{0:T(128)}, u32[]{:S(2)}) copy-start(f32[9]{0:T(128)} %constant.86.clone) | copy-start | bytes 112
  27.6 16.7 %copy-start.12 = (f32[9]{0:T(128)S(1)}, f32[9]{0:T(128)}, u32[]{:S(2)}) copy-start(f32[9]{0:T(128)} %constant.87.clone) | copy-start | bytes 112
  27.6 16.7 %copy-start.11 = (f32[9]{0:T(128)S(1)}, f32[9]{0:T(128)}, u32[]{:S(2)}) copy-start(f32[9]{0:T(128)} %constant.88.clone) | copy-start | bytes 112
  27.6 16.8 %copy-start.10 = (f32[9]{0:T(128)S(1)}, f32[9]{0:T(128)}, u32[]{:S(2)}) copy-start(f32[9]{0:T(128)} %constant.89.clone) | copy-start | bytes 112
  27.6 16.9 %copy-start.9 = (f32[9]{0:T(128)S(1)}, f32[9]{0:T(128)}, u32[]{:S(2)}) copy-start(f32[9]{0:T(128)} %constant.90.clone) | copy-start | bytes 112
  27.6 16.9 %copy-start.8 = (f32[9]{0:T(128)S(1)}, f32[9]{0:T(128)}, u32[]{:S(2)}) copy-start(f32[9]{0:T(128)} %constant.91.clone) | copy-start | bytes 112
  27.6 17.0 %copy-start.17 = (s32[1,1,32]{2,1,0:T(1,128)S(1)}, s32[1,1,32]{2,1,0:T(1,128)}, u32[]{:S(2)}) copy-start(s32[1,1,32]{2,1,0:T(1,128)} %param.33) | copy-start | bytes 388
  33.0 9.3 %collective-permute-start.8 = (f32[315,3,8]{0,2,1:T(8,128)S(1)}, f32[315,3,8]{0,2,1:T(8,128)S(1)}, u32[]{:S(2)}, u32[]{:S(2)}) collective-permute-start(f32[315,3,8]{0,2,1:T(8,128)S(1)} %get-tuple-element.108), channel_id=1, source_target_pairs={{15,0},{0,1},{1,2},{2,3},{3,4},{4,5},{5,6},{6,7},{7,8},{8,9},{9,10... | collective-permute-start | bytes 90728 | tf_op jit(solution)/shard_map/ppermute | solution.py:23
  33.0 9.2 %collective-permute-start.9 = (f32[315,3,8]{0,2,1:T(8,128)S(1)}, f32[315,3,8]{0,2,1:T(8,128)S(1)}, u32[]{:S(2)}, u32[]{:S(2)}) collective-permute-start(f32[315,3,8]{0,2,1:T(8,128)S(1)} %get-tuple-element.109), channel_id=1, source_target_pairs={{1,0},{2,1},{3,2},{4,3},{5,4},{6,5},{7,6},{8,7},{9,8},{10,9},{11,1... | collective-permute-start | bytes 90728 | tf_op jit(solution)/shard_map/ppermute | solution.py:23
  37.8 6.3 %collective-permute-start.2 = (f32[3,2,9,128]{3,2,1,0:T(8,128)S(1)}, f32[3,2,9,128]{3,2,1,0:T(8,128)S(1)}, u32[]{:S(2)}, u32[]{:S(2)}) collective-permute-start(f32[3,2,9,128]{3,2,1,0:T(8,128)S(1)} %pad_maximum_fusion.1), channel_id=1, source_target_pairs={{15,0},{0,1},{1,2},{2,3},{3,4},{4,5},{5,6},{6,7},{7,8},{8,9},{9,10... | collective-permute-start | bytes 82952 | tf_op jit(solution)/shard_map/ppermute | solution.py:23
  37.8 6.3 %collective-permute-start.3 = (f32[3,2,9,128]{3,2,1,0:T(8,128)S(1)}, f32[3,2,9,128]{3,2,1,0:T(8,128)S(1)}, u32[]{:S(2)}, u32[]{:S(2)}) collective-permute-start(f32[3,2,9,128]{3,2,1,0:T(8,128)S(1)} %pad_maximum_fusion.2), channel_id=1, source_target_pairs={{1,0},{2,1},{3,2},{4,3},{5,4},{6,5},{7,6},{8,7},{9,8},{10,9},{11,1... | collective-permute-start | bytes 82952 | tf_op jit(solution)/shard_map/ppermute | solution.py:23
  252.4 4.1 %collective-permute-start.4 = (f32[3,3,512]{2,0,1:T(4,128)S(1)}, f32[3,3,512]{2,0,1:T(4,128)S(1)}, u32[]{:S(2)}, u32[]{:S(2)}) collective-permute-start(f32[3,3,512]{2,0,1:T(4,128)S(1)} %get-tuple-element.110), channel_id=1, source_target_pairs={{16,0},{0,16},{17,1},{1,17},{18,2},{2,18},{19,3},{3,19},{20,4},{4,... | collective-permute-start | bytes 55304 | tf_op jit(solution)/shard_map/ppermute | solution.py:23
  254.4 3.8 %collective-permute-start.5 = (f32[3,3,512]{2,0,1:T(4,128)S(1)}, f32[3,3,512]{2,0,1:T(4,128)S(1)}, u32[]{:S(2)}, u32[]{:S(2)}) collective-permute-start(f32[3,3,512]{2,0,1:T(4,128)S(1)} %get-tuple-element.111), channel_id=1, source_target_pairs={{16,0},{0,16},{17,1},{1,17},{18,2},{2,18},{19,3},{3,19},{20,4},{4,... | collective-permute-start | bytes 55304 | tf_op jit(solution)/shard_map/ppermute | solution.py:23
  254.5 8.3 %collective-permute-start.10 = (f32[315,8]{0,1:T(8,128)S(1)}, f32[315,8]{0,1:T(8,128)S(1)}, u32[]{:S(2)}, u32[]{:S(2)}) collective-permute-start(f32[315,8]{0,1:T(8,128)S(1)} %get-tuple-element.122), channel_id=1, source_target_pairs={{16,0},{0,16},{17,1},{1,17},{18,2},{2,18},{19,3},{3,19},{20,4},{4,... | collective-permute-start | bytes 30248 | tf_op jit(solution)/shard_map/ppermute | solution.py:23
  256.5 6.3 %collective-permute-start.11 = (f32[315,8]{0,1:T(8,128)S(1)}, f32[315,8]{0,1:T(8,128)S(1)}, u32[]{:S(2)}, u32[]{:S(2)}) collective-permute-start(f32[315,8]{0,1:T(8,128)S(1)} %get-tuple-element.123), channel_id=1, source_target_pairs={{16,0},{0,16},{17,1},{1,17},{18,2},{2,18},{19,3},{3,19},{20,4},{4,... | collective-permute-start | bytes 30248 | tf_op jit(solution)/shard_map/ppermute | solution.py:23
  258.3 5.8 %collective-permute-start.6 = (f32[3,512]{1,0:T(4,128)S(1)}, f32[3,512]{1,0:T(4,128)S(1)}, u32[]{:S(2)}, u32[]{:S(2)}) collective-permute-start(f32[3,512]{1,0:T(4,128)S(1)} %get-tuple-element.126), channel_id=1, source_target_pairs={{15,0},{0,1},{1,2},{2,3},{3,4},{4,5},{5,6},{6,7},{7,8},{8,9},{9,10... | collective-permute-start | bytes 18440 | tf_op jit(solution)/shard_map/ppermute | solution.py:23
  258.4 5.8 %collective-permute-start.7 = (f32[3,512]{1,0:T(4,128)S(1)}, f32[3,512]{1,0:T(4,128)S(1)}, u32[]{:S(2)}, u32[]{:S(2)}) collective-permute-start(f32[3,512]{1,0:T(4,128)S(1)} %get-tuple-element.127), channel_id=1, source_target_pairs={{1,0},{2,1},{3,2},{4,3},{5,4},{6,5},{7,6},{8,7},{9,8},{10,9},{11,1... | collective-permute-start | bytes 18440 | tf_op jit(solution)/shard_map/ppermute | solution.py:23
  (6 other events, 41.3 us)
where the time goes:
time: 266 us; the launch traced here: 265 us
  other arithmetic  110 us (41%)
  matrix products  73.6 us (28%)
  local copies, waits for them, and re-layouts  30.5 us (11%)
  loops' own time  24.9 us (9%)
  starting transfers between devices  20.7 us (8%)
  waiting for transfers between devices  4.23 us (2%)
    reduce_sum x12, other arithmetic, pair_stress(): entries.append(jnp.sum(weight * entry_value, axis=2))  90.5 us
    dot_general x1, matrix products, on_device(): jnp.dot(0.5 * force, incidence, precision=highest, preferred_element_type...  68.3 us
    another operation x1, loops' own time, on_device(): lax.scan(add_slot, jnp.zeros((6, own_count, TILE), jnp.float32), jnp.aran...  24.9 us
    ppermute x12, starting transfers between devices, passed_along(): return lax.ppermute(block, axis, route)  20.7 us
    mul x12, other arithmetic, pair_stress(): weight = shear_scale * valid_weight[:, None, None] * inverse / radius_sq  7.8 us
    mul x1, local copies, waits for them, and re-layouts, moment_terms(): products[:, None, :] * monomial[None, :, :]  7.28 us
    dynamic_slice x12, local copies, waits for them, and re-layouts, on_device(): lax.scan(add_slot, jnp.zeros((6, own_count, TILE), jnp.float32), jnp.aran...  7.05 us
    gather x12, local copies, waits for them, and re-layouts, add_slot(): source_tiles = source_pool[pair_rows[:, slot_index]].transpose(1, 0, 2)  7.02 us
  transfers between devices with their start and end apart: 12, of which 3 were waited for; matrix products, arithmetic and copies ran while one was open for 10% of the time, Pallas kernels for 0%

commit v1 on v0

v1 whole, which is shorter than its diff:
```python
import functools

import jax
import jax.numpy as jnp
import numpy as np
from jax import lax
from jax.experimental import pallas as pl
from jax.experimental.pallas import tpu as pltpu
from jax.sharding import PartitionSpec as P

TILE = 128
NODE_DEV = 512
CELL_DEV = 8
core_radius = 0.1
shear_scale = 0.25
neighbour_offsets = ((-1, -1), (-1, 0), (-1, 1), (0, -1), (0, 1), (1, -1), (1, 0), (1, 1))
MONO = 35
MONO_PAD = 40
MOMENT_LANES = 384
UNROLL = 4
NODE_LOW = 256
f32 = jnp.float32
bf16 = jnp.bfloat16


def passed_along(block, axis, distance):
    size = lax.axis_size(axis)
    route = [((i - distance) % size, i) for i in range(size)]
    return lax.ppermute(block, axis, route)


def exponent_table():
    rows = []
    for degree in range(5):
        for first in range(degree, -1, -1):
            for second in range(degree - first, -1, -1):
                rows.append((first, second, degree - first - second))
    table = np.zeros((3, MONO_PAD, TILE), np.float32)
    table[:, :MONO] = np.array(rows, np.float32).T[:, :, None]
    return table


def nt_dot(left, right):
    return lax.dot_general(left, right, (((1,), (1,)), ((), ())), preferred_element_type=f32)


def two_pieces(value):
    high = value.astype(bf16)
    return high, (value - high.astype(f32)).astype(bf16)


def pack_kernel(ghost_list, ghost_count, mid, line, burgers, pool, out_x, out_up, out_down):
    tiles, slots = pool.shape[0], ghost_list.shape[1]
    for t in range(tiles):
        cols = slice(t * TILE, (t + 1) * TILE)
        b, l = burgers[:, cols], line[:, cols]
        pool[t, 0:3] = mid[:, cols] - 0.5
        pool[t, 3:4] = b[1:2] * l[2:3] - b[2:3] * l[1:2]
        pool[t, 4:5] = b[2:3] * l[0:1] - b[0:1] * l[2:3]
        pool[t, 5:6] = b[0:1] * l[1:2] - b[1:2] * l[0:1]
        pool[t, 6:8] = jnp.zeros((2, TILE), f32)
    for k in range(8):
        for g in range(slots):
            valid = jnp.where(g < ghost_count[k], 1.0, 0.0).astype(f32)
            packet = pool[ghost_list[k, g]] * valid
            if k == 3:
                out_down[g] = packet
            elif k == 4:
                out_up[g] = packet
            else:
                out_x[(k if k < 3 else k - 2) * slots + g] = packet


def moment_kernel(exponents, cell, mid, line, burgers, out, total):
    segments = mid.shape[1]
    chunk = 4 * TILE
    total[...] = jnp.zeros(total.shape, f32)

    def step(i, carry):
        start = pl.multiple_of(i * chunk, chunk)
        u = 2.0 * (mid[:, pl.ds(start, chunk)] - 0.5)
        b, l = burgers[:, pl.ds(start, chunk)], line[:, pl.ds(start, chunk)]
        parts = []
        for j in range(4):
            cols = slice(j * TILE, (j + 1) * TILE)
            value = None
            for c in range(3):
                base = u[c : c + 1, cols]
                powers = [base, base * base]
                powers += [powers[1] * base, powers[1] * powers[1]]
                power = jnp.ones((MONO_PAD, TILE), f32)
                for e in range(4):
                    power = jnp.where(exponents[c] == e + 1.0, powers[e], power)
                value = power if value is None else value * power
            parts.append(value)
        monomial = jnp.concatenate(parts, axis=1)
        rows = lax.broadcasted_iota(jnp.int32, (TILE, chunk), 0)
        member = jnp.where(rows == cell[:, pl.ds(start, chunk)], 1.0, 0.0).astype(bf16)
        for beta in range(3):
            for gamma in range(3):
                p = 3 * beta + gamma
                high, low = two_pieces(monomial * (b[beta : beta + 1] * l[gamma : gamma + 1]))
                total[p] += nt_dot(high, member) + nt_dot(low, member)
        return carry

    lax.fori_loop(0, segments // chunk, step, 0)
    joined = jnp.concatenate([total[p] for p in range(9)], axis=0)
    joined = jnp.concatenate([joined, jnp.zeros((MOMENT_LANES - 9 * MONO_PAD, TILE), f32)], axis=0)
    flipped = jnp.concatenate(
        [joined[k * TILE : (k + 1) * TILE].T for k in range(MOMENT_LANES // TILE)], axis=1
    )
    out[...] = flipped[: 9 * CELL_DEV].reshape(9, CELL_DEV, MOMENT_LANES)


def spread_fields(own, spread, tiles):
    def step(t, carry):
        columns = own[t].T
        for c in range(3):
            spread[t, c] = jnp.broadcast_to(columns[:, c : c + 1], (TILE, TILE))
        return carry

    lax.fori_loop(0, tiles, step, 0, unroll=2)


def write_features(block, features, s):
    y = [block[c : c + 1] for c in range(3)]
    g = [shear_scale * block[c + 3 : c + 4] for c in range(3)]
    ys = [shear_scale * v for v in y]
    near = g + [2.0 * y[c] * g[c] for c in range(3)]
    near += [y[a] * g[b] + y[b] * g[a] for a, b in ((0, 1), (0, 2), (1, 2))]
    near = jnp.concatenate(near + [jnp.zeros((7, TILE), f32)], axis=0)
    far = [jnp.full((1, TILE), shear_scale, f32)] + ys
    far += [y[a] * ys[b] for a, b in ((0, 0), (1, 1), (2, 2), (0, 1), (0, 2), (1, 2))]
    far = jnp.concatenate(far + [jnp.zeros((6, TILE), f32)], axis=0)
    for base, value in ((0, near), (1, far)):
        high, low = two_pieces(value)
        rows, cols = base * 32, base * 2 * TILE
        features[s, rows : rows + 16, cols : cols + TILE] = high
        features[s, rows : rows + 16, cols + TILE : cols + 2 * TILE] = high
        features[s, rows + 16 : rows + 32, cols : cols + TILE] = low
        features[s, rows + 16 : rows + 32, cols + TILE : cols + 2 * TILE] = low
        other = (1 - base) * 2 * TILE
        features[s, rows : rows + 32, other : other + 2 * TILE] = jnp.zeros((32, 2 * TILE), bf16)


def add_items(items, count, pool, features, spread, acc):
    def step(i, carry):
        results = []
        for u in range(UNROLL):
            item = items[i * UNROLL + u]
            t, s = lax.shift_right_logical(item, 6), item & 63
            block = pool[s]
            r = [spread[t, c] - block[c : c + 1] for c in range(3)]
            radius_sq = r[0] * r[0] + r[1] * r[1] + (r[2] * r[2] + core_radius**2)
            inverse = lax.rsqrt(radius_sq)
            inverse_sq = inverse * inverse
            near = inverse_sq * inverse
            p = r[0] * block[3:4] + r[1] * block[4:5] + r[2] * block[5:6]
            far = near * inverse_sq * p
            left = jnp.concatenate([*two_pieces(near), *two_pieces(far)], axis=1)
            results.append((t, nt_dot(left, features[s])))
        for t, value in results:
            acc[t] += value
        return carry

    lax.fori_loop(0, (count + UNROLL - 1) // UNROLL, step, 0)


def own_kernel(pair_list, pair_count, pool, acc, ghost_items, own_items, blocks, features, spread):
    tiles, slots = pair_list.shape

    def listing(t, positions):
        own_at, ghost_at = positions
        limit = pair_count[t]
        for n in range(slots):
            s = pair_list[t, n]
            valid = n < limit
            own_items[own_at] = t * 64 + s
            ghost_items[ghost_at + 1] = t * 64 + (s - tiles)
            own_at = own_at + jnp.where(valid & (s < tiles), 1, 0)
            ghost_at = ghost_at + jnp.where(valid & (s >= tiles), 1, 0)
        return own_at, ghost_at

    own_total, ghost_total = lax.fori_loop(0, tiles, listing, (0, 0))
    ghost_items[0] = ghost_total
    for u in range(UNROLL):
        own_items[own_total + u] = tiles

    def prepare(s, carry):
        block = pool[s]
        blocks[s] = block
        write_features(block, features, s)
        acc[s] = jnp.zeros(acc.shape[1:], f32)
        return carry

    lax.fori_loop(0, tiles, prepare, 0, unroll=2)
    blocks[tiles] = jnp.zeros((8, TILE), f32)
    features[tiles] = jnp.zeros(features.shape[1:], bf16)
    spread_fields(pool, spread, tiles)
    add_items(own_items, own_total, blocks, features, spread, acc)


def tile_force(acc_tile, x, b, l):
    flipped = acc_tile.T
    near = flipped[0:16] + flipped[16:32]
    far = flipped[32:48] + flipped[48:64]
    row = lambda block, k: block[k : k + 1]
    x = [row(x, c) for c in range(3)]
    b = [row(b, c) for c in range(3)]
    l = [row(l, c) for c in range(3)]
    g = [row(near, c) for c in range(3)]
    q0 = row(far, 0)
    q = [row(far, 1 + c) for c in range(3)]
    trace = 0.5 * (row(near, 3) + row(near, 4) + row(near, 5))
    diagonal = x[0] * g[0] + x[1] * g[1] + x[2] * g[2] - trace + 1.5 * core_radius**2 * q0
    s = []
    for k, (m, n) in enumerate(((0, 0), (1, 1), (2, 2), (0, 1), (0, 2), (1, 2))):
        value = x[m] * g[n] + x[n] * g[m] - row(near, 3 + k)
        second = x[m] * (x[n] * q0 - q[n]) - x[n] * q[m] + row(far, 4 + k)
        value = value - 3.0 * second
        s.append(value + diagonal if m == n else value)
    traction = [
        s[0] * b[0] + s[3] * b[1] + s[4] * b[2],
        s[3] * b[0] + s[1] * b[1] + s[5] * b[2],
        s[4] * b[0] + s[5] * b[1] + s[2] * b[2],
    ]
    return [
        0.5 * (traction[1] * l[2] - traction[2] * l[1]),
        0.5 * (traction[2] * l[0] - traction[0] * l[2]),
        0.5 * (traction[0] * l[1] - traction[1] * l[0]),
    ]


def ghost_kernel(merged, *refs):
    ghost_list, own, x_in, below, above, acc_in, line, burgers, node, moments = refs[:10]
    outs, (items, blocks, features, spread, acc, force, grid) = refs[10:-7], refs[-7:]
    tiles, slots = own.shape[0], x_in.shape[0] // 6
    ghosts = 8 * slots
    total = ghost_list[0]

    def copy_item(k, carry):
        items[k] = ghost_list[k + 1]
        return carry

    lax.fori_loop(0, total, copy_item, 0)
    for u in range(UNROLL):
        items[total + u] = ghosts
    groups = [(below, 1), (x_in, 4), (above, 1), (below, 0), (above, 0), (below, 2), (x_in, 1), (above, 2)]
    rows = lax.broadcasted_iota(jnp.int32, (8, TILE), 0)
    for q, (source, place) in enumerate(groups):
        a, b = neighbour_offsets[q]
        shift = jnp.where(rows == 0, float(a), jnp.where(rows == 1, float(b), 0.0))
        for g in range(slots):
            block = source[place * slots + g] + shift
            blocks[q * slots + g] = block
            write_features(block, features, q * slots + g)
    blocks[ghosts] = jnp.zeros((8, TILE), f32)
    features[ghosts] = jnp.zeros(features.shape[1:], bf16)
    spread_fields(own, spread, tiles)
    acc[...] = acc_in[...]
    add_items(items, total, blocks, features, spread, acc)

    def finish(t, carry):
        cols = pl.ds(pl.multiple_of(t * TILE, TILE), TILE)
        rows = tile_force(acc[t], own[t], burgers[:, cols], line[:, cols])
        for c in range(3):
            force[c : c + 1, cols] = rows[c]
        return carry

    lax.fori_loop(0, tiles, finish, 0, unroll=4)
    high_count = 9 * NODE_DEV // NODE_LOW
    chunk = 4 * TILE
    grid[...] = jnp.zeros(grid.shape, f32)

    def scatter(i, carry):
        cols = pl.ds(pl.multiple_of(i * chunk, chunk), chunk)
        pieces = []
        for c in range(3):
            rest = force[c : c + 1, cols]
            for k in range(3):
                piece = rest.astype(bf16).astype(f32)
                pieces.append(piece)
                rest = rest - piece
        for end in range(2):
            index = node[end : end + 1, cols]
            high, low = lax.shift_right_logical(index, 8), index & (NODE_LOW - 1)
            mask = lax.broadcasted_iota(jnp.int32, (32, chunk), 0) == high
            left = jnp.concatenate([jnp.where(mask, v, 0.0).astype(bf16) for v in pieces], axis=0)
            lows = lax.broadcasted_iota(jnp.int32, (NODE_LOW, chunk), 0)
            right = jnp.where(lows == low, 1.0, 0.0).astype(bf16)
            grid[...] += nt_dot(left, right)
        return carry

    lax.fori_loop(0, force.shape[1] // chunk, scatter, 0)
    halves = NODE_DEV // NODE_LOW
    sums = []
    for c in range(3):
        base = c * 96
        sums.append(grid[base : base + 32] + grid[base + 32 : base + 64] + grid[base + 64 : base + 96])

    def part(d):
        blocks = []
        for h in range(halves):
            k = d * halves + h
            blocks.append(jnp.concatenate([sums[c][k : k + 1] for c in range(3)] + [jnp.zeros((5, NODE_LOW), f32)], axis=0))
        return jnp.concatenate([moments[d]] + blocks, axis=1)

    for b in range(3):
        low, middle, high = part(b), part(3 + b), part(6 + b)
        outs[0][b] = middle
        if merged:
            outs[1][b] = low + high
        else:
            outs[1][b] = high
            outs[2][b] = low


def on_device(merged, seg_mid, seg_line, seg_burgers, seg_cell, seg_node, ghost_list, ghost_count, pair_list, pair_count):
    mid, line, burgers = seg_mid[0, 0], seg_line[0, 0], seg_burgers[0, 0]
    tiles, slots = mid.shape[1] // TILE, ghost_list.shape[-1]
    pairs = pair_list.shape[-1]
    vmem = pl.BlockSpec(memory_space=pltpu.VMEM)
    smem = pl.BlockSpec(memory_space=pltpu.SMEM)
    shape = jax.ShapeDtypeStruct
    params = pltpu.CompilerParams(vmem_limit_bytes=50 * 2**20)
    pool, out_x, out_up, out_down = pl.pallas_call(
        pack_kernel,
        in_specs=[smem, smem, vmem, vmem, vmem],
        out_specs=[vmem] * 4,
        out_shape=[shape((k, 8, TILE), f32) for k in (tiles, 6 * slots, slots, slots)],
        name="pack",
    )(ghost_list[0, 0], ghost_count[0, 0], mid, line, burgers)
    if merged:
        x_in = passed_along(out_x, "dx", 1)
    else:
        x_in = jnp.concatenate(
            [passed_along(out_x[: 3 * slots], "dx", -1), passed_along(out_x[3 * slots :], "dx", 1)]
        )
    pick = lambda k: x_in[k * slots : (k + 1) * slots]
    below = passed_along(jnp.concatenate([out_up, pick(5), pick(2)]), "dy", 1)
    above = passed_along(jnp.concatenate([out_down, pick(3), pick(0)]), "dy", -1)
    moments = pl.pallas_call(
        moment_kernel,
        in_specs=[vmem] * 5,
        out_specs=vmem,
        out_shape=shape((9, CELL_DEV, MOMENT_LANES), f32),
        scratch_shapes=[pltpu.VMEM((9, MONO_PAD, TILE), f32)],
        compiler_params=params,
        name="moments",
    )(jnp.asarray(exponent_table()), seg_cell[0], mid, line, burgers)
    room = tiles * pairs + 1 + UNROLL
    acc, ghost_items = pl.pallas_call(
        own_kernel,
        in_specs=[smem, smem, vmem],
        out_specs=[vmem, smem],
        out_shape=[shape((tiles, TILE, 64), f32), shape((room,), jnp.int32)],
        scratch_shapes=[
            pltpu.SMEM((room,), jnp.int32),
            pltpu.VMEM((tiles + 1, 8, TILE), f32),
            pltpu.VMEM((tiles + 1, 64, 4 * TILE), bf16),
            pltpu.VMEM((tiles, 3, TILE, TILE), f32),
        ],
        compiler_params=params,
        name="own_pairs",
    )(pair_list[0, 0], pair_count[0, 0], pool)
    width = MOMENT_LANES + NODE_DEV
    parts = pl.pallas_call(
        functools.partial(ghost_kernel, merged),
        in_specs=[smem] + [vmem] * 9,
        out_specs=[vmem] * (2 if merged else 3),
        out_shape=[shape((3, 8, width), f32)] * (2 if merged else 3),
        scratch_shapes=[
            pltpu.SMEM((room,), jnp.int32),
            pltpu.VMEM((8 * slots + 1, 8, TILE), f32),
            pltpu.VMEM((8 * slots + 1, 64, 4 * TILE), bf16),
            pltpu.VMEM((tiles, 3, TILE, TILE), f32),
            pltpu.VMEM((tiles, TILE, 64), f32),
            pltpu.VMEM((3, tiles * TILE), f32),
            pltpu.VMEM((288, NODE_LOW), f32),
        ],
        compiler_params=params,
        name="ghost_pairs",
    )(ghost_items, pool, x_in, below, above, acc, line, burgers, seg_node[0, 0], moments)
    middle = parts[0] + passed_along(parts[1], "dx", 1)
    if not merged:
        middle = middle + passed_along(parts[2], "dx", -1)
    total = middle[1] + passed_along(middle[2], "dy", 1) + passed_along(middle[0], "dy", -1)
    node_force = total[:3, MOMENT_LANES:]
    cells = total[:, : 9 * MONO_PAD].reshape(CELL_DEV, 9, MONO_PAD)[:, :, :MONO]
    return node_force[None, None], cells.reshape(CELL_DEV, 9 * MONO).T


def solution(mesh):
    in_specs = (
        P("dx", "dy", None, None),
        P("dx", "dy", None, None),
        P("dx", "dy", None, None),
        P("dx", "dy", None),
        P("dx", "dy", None, None),
        P("dx", "dy", None, None),
        P("dx", "dy", None),
        P("dx", "dy", None, None),
        P("dx", "dy", None),
    )
    out_specs = (P("dx", "dy", None, None), P(None, ("dx", "dy")))
    merged = mesh.shape["dx"] == 2
    return jax.shard_map(
        functools.partial(on_device, merged), mesh=mesh, in_specs=in_specs, out_specs=out_specs, check_vma=False
    )
```

time: 266 us -> 88.3 us (0.33)
  other arithmetic: 110 us -> 1.42 us
  matrix products: 73.6 us -> 0 us
  Pallas kernels: 0 us -> 48.4 us
  loops' own time: 24.9 us -> 0 us
  local copies, waits for them, and re-layouts: 30.5 us -> 15.4 us
  starting transfers between devices: 20.7 us -> 16.6 us
    reduce_sum x12 -> x0, other arithmetic: 90.5 us -> none  [pair_stress(): entries.append(jnp.sum(weight * entry_value, axis=2))]
    dot_general x2 -> x0, matrix products: 73.6 us -> none  [the longest x1 68.3 us: on_device(): jnp.dot(0.5 * force, incidence, precision=highest, preferred_element_type...]
    pallas_call x0 -> x4, Pallas kernels: none -> 48.4 us  [the longest x1 21.5 us: on_device(): pl.pallas_call(own_kernel, in_specs=[smem, smem, vmem], out_specs=[vmem,...]
    another operation x1 -> x0, loops' own time: 24.9 us -> none  [on_device(): lax.scan(add_slot, jnp.zeros((6, own_count, TILE), jnp.float32), jnp.aran...]
    gather x16 -> x0, local copies, waits for them, and re-layouts: 13.7 us -> none  [the longest x12 7.02 us: add_slot(): source_tiles = source_pool[pair_rows[:, slot_index]].transpose(1, 0, 2)]
    unnamed x41 -> x26, local copies, waits for them, and re-layouts: 1.71 us -> 13.3 us
    mul x16 -> x0, other arithmetic: 11.3 us -> none  [the longest x12 7.8 us: pair_stress(): weight = shear_scale * valid_weight[:, None, None] * inverse / radius_sq]
    mul x2 -> x0, local copies, waits for them, and re-layouts: 7.36 us -> none  [the longest x1 7.28 us: moment_terms(): products[:, None, :] * monomial[None, :, :]]
  transfers between devices with their start and end apart: 12 -> 6, of which waited for: 3 -> 3; matrix products, arithmetic and copies ran while one was open for 10% -> 2% of each run, Pallas kernels for 0% -> 33%
where the time goes in v1:
time: 88.3 us; the launch traced here: 88.8 us
  Pallas kernels  48.4 us (55%)
  starting transfers between devices  16.6 us (19%)
  local copies, waits for them, and re-layouts  15.4 us (17%)
  waiting for transfers between devices  6.31 us (7%)
  other arithmetic  1.42 us (2%)
    pallas_call x1, Pallas kernels, on_device(): pl.pallas_call(own_kernel, in_specs=[smem, smem, vmem], out_specs=[vmem,...  21.5 us
    pallas_call x1, Pallas kernels, on_device(): pl.pallas_call(functools.partial(ghost_kernel, merged), in_specs=[smem] +...  17.3 us
    ppermute x6, starting transfers between devices, passed_along(): return lax.ppermute(block, axis, route)  16.6 us
    unnamed x26, local copies, waits for them, and re-layouts  13.3 us
    pallas_call x1, Pallas kernels, on_device(): pl.pallas_call(moment_kernel, in_specs=[vmem] * 5, out_specs=vmem, out_sh...  7.93 us
    ppermute x6, waiting for transfers between devices, passed_along(): return lax.ppermute(block, axis, route)  6.31 us
  transfers between devices with their start and end apart: 6, of which 3 were waited for; matrix products, arithmetic and copies ran while one was open for 2% of the time, Pallas kernels for 33%

profile of v1, /device:TPU:0, one launch (start us, length us, event | category | flops | bytes accessed | tf_op | source)
XLA Modules:
  0.0 88.8 jit_solution(15581838710702124143)
XLA Ops:
  0.6 1.3 %copy.16.ghost_list = s32[8,2]{1,0:T(8,128)} copy(s32[8,2]{0,1:T(2,128)} %bitcast.35) | data formatting | bytes 128 | tf_op jit(solution)/shard_map/squeeze | solution.py:332
  2.0 1.5 %copy.24 = f32[1,1,3,4096]{3,2,1,0:T(4,128)} copy(f32[1,1,3,4096]{3,1,2,0:T(1,128)} %param.10) | data formatting | bytes 98304
  3.4 1.5 %copy_bitcast_fusion = (f32[3,4096]{1,0:T(4,128)}, f32[3,4096]{1,0:T(4,128)}) fusion(f32[1,1,3,4096]{3,1,2,0:T(1,128)} %param.12, f32[1,1,3,4096]{3,1,2,0:T(1,128)} %param.11), kind=kLoop, calls=%fused_computation | loop fusion | bytes 196608
  5.0 1.7 %pack.1 = (f32[32,8,128]{2,1,0:T(8,128)}, f32[12,8,128]{2,1,0:T(8,128)}, f32[2,8,128]{2,1,0:T(8,128)}, f32[2,8,128]{2,1,0:T(8,128)}) custom-call(s32[8,2]{1,0:T(8,128)} %copy.16.ghost_list, s32[8]{0:T(128)} %bitcast.36, f32[3,4096]{1,0:T(4,128)} %bitcast.27, f32[3,4096]{1,0:T(4,128)} %get-tuple-element.29.line.refs_6_, ...), custom_call_target="tpu_custom_call" | custom-call | tf_op jit(solution)/shard_map/pack/pallas_call | solution.py:326
  6.6 3.0 %collective-permute-start = (f32[12,8,128]{2,1,0:T(8,128)}, f32[12,8,128]{2,1,0:T(8,128)S(1)}, u32[]{:S(2)}, u32[]{:S(2)}) collective-permute-start(f32[12,8,128]{2,1,0:T(8,128)} %get-tuple-element.12), channel_id=1, source_target_pairs={{16,0},{0,16},{17,1},{1,17},{18,2},{2,18},{19,3},{3,19},{20,4},{4,... | collective-permute-start | bytes 147464 | tf_op jit(solution)/shard_map/ppermute | solution.py:29
  9.6 2.3 %collective-permute-done.refs_2_ = f32[12,8,128]{2,1,0:T(8,128)S(1)} collective-permute-done((f32[12,8,128]{2,1,0:T(8,128)}, f32[12,8,128]{2,1,0:T(8,128)S(1)}, u32[]{:S(2)}, u32[]{:S(2)}) %collective-permute-start) | collective-permute-done | bytes 49184 | tf_op jit(solution)/shard_map/ppermute | solution.py:29
  13.3 4.4 %collective-permute-start.2 = (f32[6,8,128]{2,1,0:T(8,128)S(1)}, f32[6,8,128]{2,1,0:T(8,128)S(1)}, u32[]{:S(2)}, u32[]{:S(2)}) collective-permute-start(f32[6,8,128]{2,1,0:T(8,128)S(1)} %pad_maximum_fusion.1), channel_id=1, source_target_pairs={{1,0},{2,1},{3,2},{4,3},{5,4},{6,5},{7,6},{8,7},{9,8},{10,9},{11,1... | collective-permute-start | bytes 73736 | tf_op jit(solution)/shard_map/ppermute | solution.py:29
  17.7 0.8 copy.15
  18.5 0.8 copy-done
  19.3 0.8 copy-done.2
  20.2 0.8 copy-done.4
  21.0 0.8 copy-done.7
  22.6 7.9 %moments.1.refs_9_ = f32[9,8,384]{2,1,0:T(8,128)S(1)} custom-call(f32[3,40,128]{2,1,0:T(8,128)S(1)} %copy-done.7, s32[1,4096]{1,0:T(1,128)S(1)} %bitcast.31, f32[3,4096]{1,0:T(4,128)S(1)} %bitcast.28, f32[3,4096]{1,0:T(4,128)S(1)} %copy-done.2, f32[3,4096]{1,0:T(4,128)S(1)} %copy-done), custom_call_target="tpu_custom_call" | custom-call | tf_op jit(solution)/shard_map/moments/pallas_call | solution.py:342
  30.5 0.9 %copy-done.5 = f32[32,8,128]{2,1,0:T(8,128)S(1)} copy-done((f32[32,8,128]{2,1,0:T(8,128)S(1)}, f32[32,8,128]{2,1,0:T(8,128)}, u32[]{:S(2)}) %copy-start.5) | copy-done | bytes 131096
  32.1 21.5 %own_pairs.1 = (f32[32,128,64]{2,1,0:T(8,128)S(1)}, s32[389]{0:T(512)S(1)}) custom-call(s32[32,12]{1,0:T(8,128)S(1)} %bitcast.29, s32[32]{0:T(128)S(1)} %bitcast.32, f32[32,8,128]{2,1,0:T(8,128)S(1)} %copy-done.5), custom_call_target="tpu_custom_call" | custom-call | tf_op jit(solution)/shard_map/own_pairs/pallas_call | solution.py:352
  53.6 0.8 copy-done.1
  54.4 0.8 copy-done.3
  55.3 0.9 %copy-done.6 = f32[32,8,128]{2,1,0:T(8,128)S(1)} copy-done((f32[32,8,128]{2,1,0:T(8,128)S(1)}, f32[32,8,128]{2,1,0:T(8,128)}, u32[]{:S(2)}) %copy-start.6) | copy-done | bytes 131096
  56.2 0.8 copy-done.8
  56.9 17.3 %ghost_pairs.1 = (f32[3,8,896]{2,1,0:T(8,128)S(1)}, f32[3,8,896]{2,1,0:T(8,128)S(1)}) custom-call(s32[389]{0:T(512)S(1)} %get-tuple-element.11.refs_0_, f32[32,8,128]{2,1,0:T(8,128)S(1)} %copy-done.6, f32[12,8,128]{2,1,0:T(8,128)S(1)} %collective-permute-done.refs_2_, f32[6,8,128]{2,1,0:T(8,128)S(1)} %collective-permute-done.1.refs_3_, ...), custom_call_target="tpu_custom_call" | custom-call | tf_op jit(solution)/shard_map/ghost_pairs/pallas_call | solution.py:367
  74.2 4.7 %collective-permute-start.3 = (f32[3,8,896]{2,1,0:T(8,128)S(1)}, f32[3,8,896]{2,1,0:T(8,128)S(1)}, u32[]{:S(2)}, u32[]{:S(2)}) collective-permute-start(f32[3,8,896]{2,1,0:T(8,128)S(1)} %get-tuple-element.17), channel_id=1, source_target_pairs={{16,0},{0,16},{17,1},{1,17},{18,2},{2,18},{19,3},{3,19},{20,4},{4,... | collective-permute-start | bytes 258056 | tf_op jit(solution)/shard_map/ppermute | solution.py:29
  78.9 2.5 %collective-permute-done.3 = f32[3,8,896]{2,1,0:T(8,128)S(1)} collective-permute-done((f32[3,8,896]{2,1,0:T(8,128)S(1)}, f32[3,8,896]{2,1,0:T(8,128)S(1)}, u32[]{:S(2)}, u32[]{:S(2)}) %collective-permute-start.3) | collective-permute-done | bytes 86048 | tf_op jit(solution)/shard_map/ppermute | solution.py:29
  81.4 4.4 %collective-permute-start.5 = (f32[8,896]{1,0:T(8,128)S(1)}, f32[8,896]{1,0:T(8,128)S(1)}, u32[]{:S(2)}, u32[]{:S(2)}) collective-permute-start(f32[8,896]{1,0:T(8,128)S(1)} %get-tuple-element.23), channel_id=1, source_target_pairs={{1,0},{2,1},{3,2},{4,3},{5,4},{6,5},{7,6},{8,7},{9,8},{10,9},{11,1... | collective-permute-start | bytes 86024 | tf_op jit(solution)/shard_map/ppermute | solution.py:29
  85.9 1.5 %collective-permute-done.4 = f32[8,896]{1,0:T(8,128)S(1)} collective-permute-done((f32[8,896]{1,0:T(8,128)S(1)}, f32[8,896]{1,0:T(8,128)S(1)}, u32[]{:S(2)}, u32[]{:S(2)}) %collective-permute-start.4) | collective-permute-done | bytes 28704 | tf_op jit(solution)/shard_map/ppermute | solution.py:29
  (29 shorter events, 4.3 us)
Async XLA Ops:
  6.6 5.2 %collective-permute-start = (f32[12,8,128]{2,1,0:T(8,128)}, f32[12,8,128]{2,1,0:T(8,128)S(1)}, u32[]{:S(2)}, u32[]{:S(2)}) collective-permute-start(f32[12,8,128]{2,1,0:T(8,128)} %get-tuple-element.12), channel_id=1, source_target_pairs={{16,0},{0,16},{17,1},{1,17},{18,2},{2,18},{19,3},{3,19},{20,4},{4,... | collective-permute-start | bytes 147464 | tf_op jit(solution)/shard_map/ppermute | solution.py:29
  12.6 41.0 %collective-permute-start.1 = (f32[6,8,128]{2,1,0:T(8,128)S(1)}, f32[6,8,128]{2,1,0:T(8,128)S(1)}, u32[]{:S(2)}, u32[]{:S(2)}) collective-permute-start(f32[6,8,128]{2,1,0:T(8,128)S(1)} %pad_maximum_fusion), channel_id=1, source_target_pairs={{15,0},{0,1},{1,2},{2,3},{3,4},{4,5},{5,6},{6,7},{7,8},{8,9},{9,10... | collective-permute-start | bytes 73736 | tf_op jit(solution)/shard_map/ppermute | solution.py:29
  13.3 40.3 %collective-permute-start.2 = (f32[6,8,128]{2,1,0:T(8,128)S(1)}, f32[6,8,128]{2,1,0:T(8,128)S(1)}, u32[]{:S(2)}, u32[]{:S(2)}) collective-permute-start(f32[6,8,128]{2,1,0:T(8,128)S(1)} %pad_maximum_fusion.1), channel_id=1, source_target_pairs={{1,0},{2,1},{3,2},{4,3},{5,4},{6,5},{7,6},{8,7},{9,8},{10,9},{11,1... | collective-permute-start | bytes 73736 | tf_op jit(solution)/shard_map/ppermute | solution.py:29
  18.5 0.8 copy-start
  19.3 0.8 copy-start.2
  20.2 0.8 copy-start.4
  21.0 0.8 copy-start.7
  21.8 0.7 copy-start.9
  30.5 0.9 %copy-start.5 = (f32[32,8,128]{2,1,0:T(8,128)S(1)}, f32[32,8,128]{2,1,0:T(8,128)}, u32[]{:S(2)}) copy-start(f32[32,8,128]{2,1,0:T(8,128)} %get-tuple-element.10.pool.refs_1_) | copy-start | bytes 393220
  31.4 0.7 copy-start.10
  53.6 0.8 copy-start.1
  54.4 0.8 copy-start.3
  55.3 0.9 %copy-start.6 = (f32[32,8,128]{2,1,0:T(8,128)S(1)}, f32[32,8,128]{2,1,0:T(8,128)}, u32[]{:S(2)}) copy-start(f32[32,8,128]{2,1,0:T(8,128)} %get-tuple-element.10.pool.refs_1_) | copy-start | bytes 393220
  56.2 0.8 copy-start.8
  74.2 7.1 %collective-permute-start.3 = (f32[3,8,896]{2,1,0:T(8,128)S(1)}, f32[3,8,896]{2,1,0:T(8,128)S(1)}, u32[]{:S(2)}, u32[]{:S(2)}) collective-permute-start(f32[3,8,896]{2,1,0:T(8,128)S(1)} %get-tuple-element.17), channel_id=1, source_target_pairs={{16,0},{0,16},{17,1},{1,17},{18,2},{2,18},{19,3},{3,19},{20,4},{4,... | collective-permute-start | bytes 258056 | tf_op jit(solution)/shard_map/ppermute | solution.py:29
  81.4 6.0 %collective-permute-start.4 = (f32[8,896]{1,0:T(8,128)S(1)}, f32[8,896]{1,0:T(8,128)S(1)}, u32[]{:S(2)}, u32[]{:S(2)}) collective-permute-start(f32[8,896]{1,0:T(8,128)S(1)} %get-tuple-element.22), channel_id=1, source_target_pairs={{15,0},{0,1},{1,2},{2,3},{3,4},{4,5},{5,6},{6,7},{7,8},{8,9},{9,10... | collective-permute-start | bytes 86024 | tf_op jit(solution)/shard_map/ppermute | solution.py:29
  81.4 6.0 %collective-permute-start.5 = (f32[8,896]{1,0:T(8,128)S(1)}, f32[8,896]{1,0:T(8,128)S(1)}, u32[]{:S(2)}, u32[]{:S(2)}) collective-permute-start(f32[8,896]{1,0:T(8,128)S(1)} %get-tuple-element.23), channel_id=1, source_target_pairs={{1,0},{2,1},{3,2},{4,3},{5,4},{6,5},{7,6},{8,7},{9,8},{10,9},{11,1... | collective-permute-start | bytes 86024 | tf_op jit(solution)/shard_map/ppermute | solution.py:29

commit v2 on v1

v2 whole, which is shorter than its diff:
```python
import functools

import jax
import jax.numpy as jnp
import numpy as np
from jax import lax
from jax.experimental import pallas as pl
from jax.experimental.pallas import tpu as pltpu
from jax.sharding import PartitionSpec as P

TILE = 128
NODE_DEV = 512
CELL_DEV = 8
core_radius = 0.1
shear_scale = 0.25
neighbour_offsets = ((-1, -1), (-1, 0), (-1, 1), (0, -1), (0, 1), (1, -1), (1, 0), (1, 1))
MONO = 35
MONO_PAD = 40
MOMENT_LANES = 384
UNROLL = 8
NODE_LOW = 256
f32 = jnp.float32
bf16 = jnp.bfloat16


def passed_along(block, axis, distance):
    size = lax.axis_size(axis)
    route = [((i - distance) % size, i) for i in range(size)]
    return lax.ppermute(block, axis, route)


def exponent_table():
    rows = []
    for degree in range(5):
        for first in range(degree, -1, -1):
            for second in range(degree - first, -1, -1):
                rows.append((first, second, degree - first - second))
    table = np.zeros((3, MONO_PAD, TILE), np.float32)
    table[:, :MONO] = np.array(rows, np.float32).T[:, :, None]
    return table


def nt_dot(left, right):
    return lax.dot_general(left, right, (((1,), (1,)), ((), ())), preferred_element_type=f32)


def two_pieces(value):
    high = value.astype(bf16)
    return high, (value - high.astype(f32)).astype(bf16)


def cross(b, l):
    return [b[1] * l[2] - b[2] * l[1], b[2] * l[0] - b[0] * l[2], b[0] * l[1] - b[1] * l[0]]


def pack_kernel(ghost_list, ghost_count, mid, line, burgers, out_x, out_up, out_down):
    slots = ghost_list.shape[0]
    for k in range(8):
        for g in range(slots):
            valid = jnp.where(g < ghost_count[0, k], 1.0, 0.0).astype(f32)
            at = pl.ds(ghost_list[g, k], 1)
            rows = [mid[c, at] - 0.5 for c in range(3)]
            rows += cross([burgers[c, at] for c in range(3)], [line[c, at] for c in range(3)])
            packet = jnp.concatenate(rows + [jnp.zeros((2, TILE), f32)], axis=0) * valid
            if k == 3:
                out_down[g] = packet
            elif k == 4:
                out_up[g] = packet
            else:
                out_x[(k if k < 3 else k - 2) * slots + g] = packet


def moment_kernel(exponents, cell, mid, line, burgers, out, total):
    chunks = mid.shape[1] // 4
    total[...] = jnp.zeros(total.shape, f32)
    half = total.shape[0] // 2

    def step(i, carry):
        places = [pl.ds(4 * i + j, 1) for j in range(4)]
        wide = lambda ref, c: jnp.concatenate([ref[c, at] for at in places], axis=1)
        b, l = [wide(burgers, c) for c in range(3)], [wide(line, c) for c in range(3)]
        parts = []
        for at in places:
            value = None
            for c in range(3):
                base = 2.0 * (mid[c, at] - 0.5)
                powers = [base, base * base]
                powers += [powers[1] * base, powers[1] * powers[1]]
                power = jnp.ones((MONO_PAD, TILE), f32)
                for e in range(4):
                    power = jnp.where(exponents[c] == e + 1.0, powers[e], power)
                value = power if value is None else value * power
            parts.append(value)
        monomial = jnp.concatenate(parts, axis=1)
        rows = lax.broadcasted_iota(jnp.int32, (TILE, 4 * TILE), 0)
        cells = jnp.concatenate([cell[at] for at in places], axis=1)
        member = jnp.where(rows == cells, 1.0, 0.0).astype(bf16)
        terms = [monomial * (b[p // 3] * l[p % 3]) for p in range(9)]
        terms = jnp.concatenate(terms + [jnp.zeros((half - 9 * MONO_PAD, 4 * TILE), f32)], axis=0)
        total[...] += nt_dot(jnp.concatenate(two_pieces(terms), axis=0), member)
        return carry

    lax.fori_loop(0, chunks, step, 0)
    joined = total[:half] + total[half:]
    joined = [joined[p * MONO_PAD : p * MONO_PAD + MONO] for p in range(9)]
    joined = jnp.concatenate(joined + [jnp.zeros((MOMENT_LANES - 9 * MONO, TILE), f32)], axis=0)
    flipped = jnp.concatenate(
        [joined[k * TILE : (k + 1) * TILE].T for k in range(MOMENT_LANES // TILE)], axis=1
    )
    out[...] = flipped[: 9 * CELL_DEV].reshape(9, CELL_DEV, MOMENT_LANES)


def prepare_kernel(pair_list, pair_count, mid, items, spread):
    slots, _, tiles = pair_list.shape

    def listing(t, at):
        for n in range(slots):
            items[at + n + 1] = t * 64 + pair_list[n, 0, t]
        return at + pair_count[0, t]

    items[0] = lax.fori_loop(0, tiles, listing, 0, unroll=2)

    def widen(t, carry):
        rows = [mid[c, pl.ds(t, 1)] - 0.5 for c in range(3)]
        columns = jnp.concatenate(rows + [jnp.zeros((5, TILE), f32)], axis=0).T
        for c in range(3):
            spread[t, c] = jnp.broadcast_to(columns[:, c : c + 1], (TILE, TILE))
        return carry

    lax.fori_loop(0, tiles, widen, 0, unroll=4)


def write_features(source, features, s):
    y = [source[c, pl.ds(s, 1)] for c in range(3)]
    g = [shear_scale * source[c + 3, pl.ds(s, 1)] for c in range(3)]
    ys = [shear_scale * v for v in y]
    near = g + [2.0 * y[c] * g[c] for c in range(3)]
    near += [y[a] * g[b] + y[b] * g[a] for a, b in ((0, 1), (0, 2), (1, 2))]
    near = jnp.concatenate(near + [jnp.zeros((7, TILE), f32)], axis=0)
    far = [jnp.full((1, TILE), shear_scale, f32)] + ys
    far += [y[a] * ys[b] for a, b in ((0, 0), (1, 1), (2, 2), (0, 1), (0, 2), (1, 2))]
    far = jnp.concatenate(far + [jnp.zeros((6, TILE), f32)], axis=0)
    for base, value in ((0, near), (1, far)):
        high, low = two_pieces(value)
        rows, cols = base * 32, base * 2 * TILE
        features[s, rows : rows + 16, cols : cols + TILE] = high
        features[s, rows : rows + 16, cols + TILE : cols + 2 * TILE] = high
        features[s, rows + 16 : rows + 32, cols : cols + TILE] = low
        features[s, rows + 16 : rows + 32, cols + TILE : cols + 2 * TILE] = low
        other = (1 - base) * 2 * TILE
        features[s, rows : rows + 32, other : other + 2 * TILE] = jnp.zeros((32, 2 * TILE), bf16)


def add_items(items, count, source, features, spread, acc):
    def step(i, carry):
        results = []
        for u in range(UNROLL):
            item = items[i * UNROLL + u + 1]
            t, s = lax.shift_right_logical(item, 6), item & 63
            y = [source[c, pl.ds(s, 1)] for c in range(6)]
            r = [spread[t, c] - y[c] for c in range(3)]
            radius_sq = r[0] * r[0] + r[1] * r[1] + (r[2] * r[2] + core_radius**2)
            inverse = lax.rsqrt(radius_sq)
            inverse_sq = inverse * inverse
            near = inverse_sq * inverse
            p = r[0] * y[3] + r[1] * y[4] + r[2] * y[5]
            far = near * inverse_sq * p
            left = jnp.concatenate([*two_pieces(near), *two_pieces(far)], axis=1)
            results.append((t, nt_dot(left, features[s])))
        for t, value in results:
            acc[t] += value
        return carry

    lax.fori_loop(0, (count + UNROLL - 1) // UNROLL, step, 0)


def tile_force(acc_tile, x, b, l):
    flipped = acc_tile.T
    near = flipped[0:16] + flipped[16:32]
    far = flipped[32:48] + flipped[48:64]
    row = lambda block, k: block[k : k + 1]
    g = [row(near, c) for c in range(3)]
    q0 = row(far, 0)
    q = [row(far, 1 + c) for c in range(3)]
    trace = 0.5 * (row(near, 3) + row(near, 4) + row(near, 5))
    diagonal = x[0] * g[0] + x[1] * g[1] + x[2] * g[2] - trace + 1.5 * core_radius**2 * q0
    s = []
    for k, (m, n) in enumerate(((0, 0), (1, 1), (2, 2), (0, 1), (0, 2), (1, 2))):
        value = x[m] * g[n] + x[n] * g[m] - row(near, 3 + k)
        second = x[m] * (x[n] * q0 - q[n]) - x[n] * q[m] + row(far, 4 + k)
        value = value - 3.0 * second
        s.append(value + diagonal if m == n else value)
    traction = [
        s[0] * b[0] + s[3] * b[1] + s[4] * b[2],
        s[3] * b[0] + s[1] * b[1] + s[5] * b[2],
        s[4] * b[0] + s[5] * b[1] + s[2] * b[2],
    ]
    return [
        0.5 * (traction[1] * l[2] - traction[2] * l[1]),
        0.5 * (traction[2] * l[0] - traction[0] * l[2]),
        0.5 * (traction[0] * l[1] - traction[1] * l[0]),
    ]


def pair_kernel(merged, *refs):
    item_list, spread, mid, line, burgers, x_in, below, above, node, moments = refs[:10]
    outs, (items, source, features, acc, force, grid) = refs[10:-6], refs[-6:]
    tiles, slots = mid.shape[1], x_in.shape[0] // 6
    pool = tiles + 8 * slots
    total = item_list[0]

    def copy_items(k, carry):
        for u in range(8):
            items[k * 8 + u + 1] = item_list[k * 8 + u + 1]
        return carry

    lax.fori_loop(0, (total + 7) // 8, copy_items, 0)
    for u in range(UNROLL):
        items[total + u + 1] = pool
    for c in range(3):
        source[c, 0:tiles] = mid[c] - 0.5
    product = cross([burgers[c] for c in range(3)], [line[c] for c in range(3)])
    for c in range(3):
        source[c + 3, 0:tiles] = product[c]
    for c in range(6):
        source[c, pool : pool + 1] = jnp.zeros((1, TILE), f32)
    groups = [(below, 1), (x_in, 4), (above, 1), (below, 0), (above, 0), (below, 2), (x_in, 1), (above, 2)]
    for q, (arrived, place) in enumerate(groups):
        shift = neighbour_offsets[q] + (0,) * 4
        for g in range(slots):
            at = tiles + q * slots + g
            for c in range(6):
                source[c, at : at + 1] = arrived[place * slots + g, c : c + 1] + float(shift[c])

    def prepare(s, carry):
        write_features(source, features, s)
        return carry

    lax.fori_loop(0, pool, prepare, 0, unroll=2)
    features[pool] = jnp.zeros(features.shape[1:], bf16)

    def clear(t, carry):
        acc[t] = jnp.zeros(acc.shape[1:], f32)
        return carry

    lax.fori_loop(0, tiles, clear, 0)
    add_items(items, total, source, features, spread, acc)

    def finish(t, carry):
        at = pl.ds(t, 1)
        pick = lambda ref: [ref[c, at] for c in range(3)]
        rows = tile_force(acc[t], pick(source), pick(burgers), pick(line))
        for c in range(3):
            force[c, at] = rows[c]
        return carry

    lax.fori_loop(0, tiles, finish, 0, unroll=4)
    chunk = 4 * TILE
    grid[...] = jnp.zeros(grid.shape, f32)

    def scatter(i, carry):
        pieces = []
        for c in range(3):
            rest = jnp.concatenate([force[c, pl.ds(4 * i + j, 1)] for j in range(4)], axis=1)
            for k in range(3):
                piece = rest.astype(bf16).astype(f32)
                pieces.append(piece)
                rest = rest - piece
        for end in range(2):
            index = node[end : end + 1, pl.ds(pl.multiple_of(i * chunk, chunk), chunk)]
            high, low = lax.shift_right_logical(index, 8), index & (NODE_LOW - 1)
            mask = lax.broadcasted_iota(jnp.int32, (32, chunk), 0) == high
            left = jnp.concatenate([jnp.where(mask, v, 0.0).astype(bf16) for v in pieces], axis=0)
            lows = lax.broadcasted_iota(jnp.int32, (NODE_LOW, chunk), 0)
            right = jnp.where(lows == low, 1.0, 0.0).astype(bf16)
            grid[...] += nt_dot(left, right)
        return carry

    lax.fori_loop(0, tiles // 4, scatter, 0)
    halves = NODE_DEV // NODE_LOW
    sums = []
    for c in range(3):
        base = c * 96
        sums.append(grid[base : base + 32] + grid[base + 32 : base + 64] + grid[base + 64 : base + 96])

    def part(d):
        blocks = []
        for h in range(halves):
            k = d * halves + h
            blocks.append(jnp.concatenate([sums[c][k : k + 1] for c in range(3)] + [jnp.zeros((5, NODE_LOW), f32)], axis=0))
        return jnp.concatenate([moments[d]] + blocks, axis=1)

    for b in range(3):
        low, middle, high = part(b), part(3 + b), part(6 + b)
        outs[0][b] = middle
        if merged:
            outs[1][b] = low + high
        else:
            outs[1][b] = high
            outs[2][b] = low


def finish_kernel(middle, first, second, node_force, cells):
    total = middle[1] + first[...] + second[...]
    cells[...] = total[:, : cells.shape[1]]
    for k in range(NODE_DEV // TILE):
        at = MOMENT_LANES + k * TILE
        node_force[:, k : k + 1] = total[:3, at : at + TILE].reshape(3, 1, TILE)


def on_device(merged, seg_mid, seg_line, seg_burgers, seg_cell, seg_node, ghost_list, ghost_count, pair_list, pair_count):
    tiles, slots = seg_mid.shape[-1] // TILE, ghost_list.shape[-1]
    mid, line, burgers = [v.reshape(3, tiles, TILE) for v in (seg_mid, seg_line, seg_burgers)]
    cell = seg_cell.reshape(tiles, TILE)
    pairs = pair_list.shape[-1]
    plain = pl.BlockSpec()
    vmem = pl.BlockSpec(memory_space=pltpu.VMEM)
    smem = pl.BlockSpec(memory_space=pltpu.SMEM)
    shape = jax.ShapeDtypeStruct
    params = pltpu.CompilerParams(vmem_limit_bytes=32 * 2**20)
    cost = lambda flops: pl.CostEstimate(flops=flops, transcendentals=0, bytes_accessed=0)
    out_x, out_up, out_down = pl.pallas_call(
        pack_kernel,
        in_specs=[smem, smem] + [plain] * 3,
        out_specs=[plain] * 3,
        out_shape=[shape((k, 8, TILE), f32) for k in (6 * slots, slots, slots)],
        compiler_params=params,
        name="pack",
    )(ghost_list[0, 0].T, ghost_count[0], mid, line, burgers)
    if merged:
        x_in = passed_along(out_x, "dx", 1)
    else:
        x_in = jnp.concatenate(
            [passed_along(out_x[: 3 * slots], "dx", -1), passed_along(out_x[3 * slots :], "dx", 1)]
        )
    pick = lambda k: x_in[k * slots : (k + 1) * slots]
    below = passed_along(jnp.concatenate([out_up, pick(5), pick(2)]), "dy", 1)
    above = passed_along(jnp.concatenate([out_down, pick(3), pick(0)]), "dy", -1)
    moments = pl.pallas_call(
        moment_kernel,
        in_specs=[plain] * 5,
        out_specs=plain,
        out_shape=shape((9, CELL_DEV, MOMENT_LANES), f32),
        scratch_shapes=[pltpu.VMEM((736, TILE), f32)],
        compiler_params=params,
        cost_estimate=cost(3 * 10**9),
        name="moments",
    )(jnp.asarray(exponent_table()), cell, mid, line, burgers)
    room = tiles * pairs + 16
    item_list, spread = pl.pallas_call(
        prepare_kernel,
        in_specs=[smem, smem, plain],
        out_specs=[smem, vmem],
        out_shape=[shape((room,), jnp.int32), shape((tiles, 3, TILE, TILE), f32)],
        compiler_params=params,
        cost_estimate=cost(3 * 10**9),
        name="prepare",
    )(pair_list[0].transpose(2, 0, 1), pair_count[0], mid)
    width = MOMENT_LANES + NODE_DEV
    count = 2 if merged else 3
    pool = tiles + 8 * slots
    parts = pl.pallas_call(
        functools.partial(pair_kernel, merged),
        in_specs=[smem, vmem] + [plain] * 8,
        out_specs=[plain] * count,
        out_shape=[shape((3, 8, width), f32)] * count,
        scratch_shapes=[
            pltpu.SMEM((room,), jnp.int32),
            pltpu.VMEM((6, pool + 1, TILE), f32),
            pltpu.VMEM((pool + 1, 64, 4 * TILE), bf16),
            pltpu.VMEM((tiles, TILE, 64), f32),
            pltpu.VMEM((3, tiles, TILE), f32),
            pltpu.VMEM((288, NODE_LOW), f32),
        ],
        compiler_params=params,
        cost_estimate=cost(10**10),
        name="pairs",
    )(item_list, spread, mid, line, burgers, x_in, below, above, seg_node[0, 0], moments)
    middle = parts[0] + passed_along(parts[1], "dx", 1)
    if not merged:
        middle = middle + passed_along(parts[2], "dx", -1)
    node_force, cells = pl.pallas_call(
        finish_kernel,
        in_specs=[plain] * 3,
        out_specs=[plain] * 2,
        out_shape=[shape((3, NODE_DEV // TILE, TILE), f32), shape((CELL_DEV, 9 * MONO), f32)],
        compiler_params=params,
        name="finish",
    )(middle, passed_along(middle[2], "dy", 1), passed_along(middle[0], "dy", -1))
    return node_force.reshape(1, 1, 3, NODE_DEV), cells.T


def solution(mesh):
    in_specs = (
        P("dx", "dy", None, None),
        P("dx", "dy", None, None),
        P("dx", "dy", None, None),
        P("dx", "dy", None),
        P("dx", "dy", None, None),
        P("dx", "dy", None, None),
        P("dx", "dy", None),
        P("dx", "dy", None, None),
        P("dx", "dy", None),
    )
    out_specs = (P("dx", "dy", None, None), P(None, ("dx", "dy")))
    merged = mesh.shape["dx"] == 2
    return jax.shard_map(
        functools.partial(on_device, merged), mesh=mesh, in_specs=in_specs, out_specs=out_specs, check_vma=False
    )
```

time: 88.3 us -> 59.5 us (0.67)
  Pallas kernels: 48.4 us -> 33.7 us
  local copies, waits for them, and re-layouts: 15.4 us -> 6.92 us
  starting transfers between devices: 16.6 us -> 8.14 us
  waiting for transfers between devices: 6.31 us -> 10 us
  other arithmetic: 1.42 us -> 0.02 us
    pallas_call x4 -> x5, Pallas kernels: 48.4 us -> 33.7 us  [the longest x1 23.6 us: on_device(): pl.pallas_call(functools.partial(pair_kernel, merged), in_specs=[smem, vm...]
    ppermute x6, starting transfers between devices: 16.6 us -> 8.14 us  [passed_along(): return lax.ppermute(block, axis, route)]
    unnamed x26 -> x30, local copies, waits for them, and re-layouts: 13.3 us -> 6.9 us
    ppermute x6, waiting for transfers between devices: 6.31 us -> 10 us  [passed_along(): return lax.ppermute(block, axis, route)]
    squeeze x2 -> x1, local copies, waits for them, and re-layouts: 1.35 us -> 0.01 us  [on_device(): middle[0]]
  transfers between devices with their start and end apart: 6 -> 6, of which waited for: 3 -> 3; matrix products, arithmetic and copies ran while one was open for 2% -> 0% of each run, Pallas kernels for 33% -> 15%
where the time goes in v2:
time: 59.5 us; the launch traced here: 59.6 us
  Pallas kernels  33.7 us (57%)
  waiting for transfers between devices  10 us (17%)
  starting transfers between devices  8.14 us (14%)
  local copies, waits for them, and re-layouts  6.92 us (12%)
  between operations  0.82 us (1%)
    pallas_call x1, Pallas kernels, on_device(): pl.pallas_call(functools.partial(pair_kernel, merged), in_specs=[smem, vm...  23.6 us
    ppermute x6, waiting for transfers between devices, passed_along(): return lax.ppermute(block, axis, route)  10 us
    ppermute x6, starting transfers between devices, passed_along(): return lax.ppermute(block, axis, route)  8.14 us
    unnamed x30, local copies, waits for them, and re-layouts  6.9 us
    pallas_call x1, Pallas kernels, on_device(): pl.pallas_call(prepare_kernel, in_specs=[smem, smem, plain], out_specs=[s...  5.25 us
    pallas_call x1, Pallas kernels, on_device(): pl.pallas_call(moment_kernel, in_specs=[plain] * 5, out_specs=plain, out_...  3.52 us
  transfers between devices with their start and end apart: 6, of which 3 were waited for; matrix products, arithmetic and copies ran while one was open for 0% of the time, Pallas kernels for 15%

profile of v2, /device:TPU:0, one launch (start us, length us, event | category | flops | bytes accessed | tf_op | source)
XLA Modules:
  0.0 59.6 jit_solution(6403198830254828984)
XLA Ops:
  0.7 0.8 %copy-done = f32[1,1,3,4096]{3,1,2,0:T(1,128)S(1)} copy-done((f32[1,1,3,4096]{3,1,2,0:T(1,128)S(1)}, f32[1,1,3,4096]{3,1,2,0:T(1,128)}, u32[]{:S(2)}) %copy-start) | copy-done | bytes 49176
  1.5 0.8 %copy-done.2 = f32[1,1,3,4096]{3,1,2,0:T(1,128)S(1)} copy-done((f32[1,1,3,4096]{3,1,2,0:T(1,128)S(1)}, f32[1,1,3,4096]{3,1,2,0:T(1,128)}, u32[]{:S(2)}) %copy-start.2) | copy-done | bytes 49176
  2.3 0.8 %copy-done.5 = f32[1,1,3,4096]{3,1,2,0:T(1,128)S(1)} copy-done((f32[1,1,3,4096]{3,1,2,0:T(1,128)S(1)}, f32[1,1,3,4096]{3,1,2,0:T(1,128)}, u32[]{:S(2)}) %copy-start.5) | copy-done | bytes 49176
  3.1 0.7 %copy-done.8 = s32[1,1,8,2]{2,3,1,0:T(2,128)S(1)} copy-done((s32[1,1,8,2]{2,3,1,0:T(2,128)S(1)}, s32[1,1,8,2]{2,3,1,0:T(2,128)}, u32[]{:S(2)}) %copy-start.8) | copy-done | bytes 88
  3.7 0.7 %copy-done.9 = s32[1,1,8]{2,1,0:T(1,128)S(1)} copy-done((s32[1,1,8]{2,1,0:T(1,128)S(1)}, s32[1,1,8]{2,1,0:T(1,128)}, u32[]{:S(2)}) %copy-start.9) | copy-done | bytes 56
  4.4 0.6 %pack.1 = (f32[12,8,128]{2,1,0:T(8,128)S(1)}, f32[2,8,128]{2,1,0:T(8,128)S(1)}, f32[2,8,128]{2,1,0:T(8,128)S(1)}) custom-call(s32[2,8]{1,0:T(2,128)S(1)} %bitcast.29, s32[1,8]{1,0:T(1,128)S(1)} %bitcast.30, f32[3,32,128]{2,1,0:T(8,128)S(1)} %bitcast.19, f32[3,32,128]{2,1,0:T(8,128)S(1)} %bitcast.23, f32[3,32,128]{2,1,0:T(8,128)S(1)} %bitcast.26), custom_call_target="tpu_custom_call" | custom-call | tf_op jit(solution)/shard_map/pack/pallas_call | solution.py:322
  5.0 3.0 %collective-permute-start = (f32[12,8,128]{2,1,0:T(8,128)S(1)}, f32[12,8,128]{2,1,0:T(8,128)S(1)}, u32[]{:S(2)}, u32[]{:S(2)}) collective-permute-start(f32[12,8,128]{2,1,0:T(8,128)S(1)} %get-tuple-element.13), channel_id=1, source_target_pairs={{16,0},{0,16},{17,1},{1,17},{18,2},{2,18},{19,3},{3,19},{20,4},{4,... | collective-permute-start | bytes 147464 | tf_op jit(solution)/shard_map/ppermute | solution.py:29
  8.1 0.8 %copy-done.3 = f32[1,1,3,4096]{3,1,2,0:T(1,128)S(1)} copy-done((f32[1,1,3,4096]{3,1,2,0:T(1,128)S(1)}, f32[1,1,3,4096]{3,1,2,0:T(1,128)}, u32[]{:S(2)}) %copy-start.3) | copy-done | bytes 49176
  8.9 0.8 %copy-done.6 = f32[1,1,3,4096]{3,1,2,0:T(1,128)S(1)} copy-done((f32[1,1,3,4096]{3,1,2,0:T(1,128)S(1)}, f32[1,1,3,4096]{3,1,2,0:T(1,128)}, u32[]{:S(2)}) %copy-start.6) | copy-done | bytes 49176
  9.7 0.7 %copy-done.11 = s32[1,1,4096]{2,1,0:T(1,128)S(1)} copy-done((s32[1,1,4096]{2,1,0:T(1,128)S(1)}, s32[1,1,4096]{2,1,0:T(1,128)}, u32[]{:S(2)}) %copy-start.11) | copy-done | bytes 16408
  10.4 0.8 %copy-done.14 = f32[3,40,128]{2,1,0:T(8,128)S(1)} copy-done((f32[3,40,128]{2,1,0:T(8,128)S(1)}, f32[3,40,128]{2,1,0:T(8,128)}, u32[]{:S(2)}) %copy-start.14) | copy-done | bytes 61464
  11.2 3.5 %moments.1.refs_9_ = f32[9,8,384]{2,1,0:T(8,128)S(1)} custom-call(f32[3,40,128]{2,1,0:T(8,128)S(1)} %copy-done.14, s32[32,128]{1,0:T(8,128)S(1)} %bitcast.32, f32[3,32,128]{2,1,0:T(8,128)S(1)} %bitcast.20, f32[3,32,128]{2,1,0:T(8,128)S(1)} %bitcast.24, f32[3,32,128]{2,1,0:T(8,128)S(1)} %bitcast.27), custom_call_target="tpu_custom_call" | custom-call | flops 3000000000 | tf_op jit(solution)/shard_map/moments/pallas_call | solution.py:339
  14.8 0.0 copy-start.7
  14.8 0.1 collective-permute-start.1
  14.9 4.4 %collective-permute-start.2 = (f32[6,8,128]{2,1,0:T(8,128)S(1)}, f32[6,8,128]{2,1,0:T(8,128)S(1)}, u32[]{:S(2)}, u32[]{:S(2)}) collective-permute-start(f32[6,8,128]{2,1,0:T(8,128)S(1)} %pad_maximum_fusion.1), channel_id=1, source_target_pairs={{1,0},{2,1},{3,2},{4,3},{5,4},{6,5},{7,6},{8,7},{9,8},{10,9},{11,1... | collective-permute-start | bytes 73736 | tf_op jit(solution)/shard_map/ppermute | solution.py:29
  19.3 5.2 %prepare.1 = (s32[400]{0:T(512)S(1)}, f32[32,3,128,128]{3,2,1,0:T(8,128)S(1)}) custom-call(s32[12,1,32]{2,1,0:T(1,128)S(1)} %bitcast.33, s32[1,32]{1,0:T(1,128)S(1)} %bitcast.34, f32[3,32,128]{2,1,0:T(8,128)S(1)} %bitcast.21), custom_call_target="tpu_custom_call" | custom-call | flops 3000000000 | tf_op jit(solution)/shard_map/prepare/pallas_call | solution.py:350
  24.6 23.6 %pairs.1 = (f32[3,8,896]{2,1,0:T(8,128)S(1)}, f32[3,8,896]{2,1,0:T(8,128)S(1)}) custom-call(s32[400]{0:T(512)S(1)} %get-tuple-element.11.refs_0_, f32[32,3,128,128]{3,2,1,0:T(8,128)S(1)} %get-tuple-element.12.refs_1_, f32[3,32,128]{2,1,0:T(8,128)S(1)} %bitcast.22, f32[3,32,128]{2,1,0:T(8,128)S(1)} %bitcast.25, f32[3,32,128]{2,1,0:T(8,128)S(1)} %bitcast.28, ...), custom_call_target="tpu_custom_call" | custom-call | flops 10000000000 | tf_op jit(solution)/shard_map/pairs/pallas_call | solution.py:362
  48.3 0.1 collective-permute-start.3
  48.4 4.5 %collective-permute-done.3 = f32[3,8,896]{2,1,0:T(8,128)S(1)} collective-permute-done((f32[3,8,896]{2,1,0:T(8,128)S(1)}, f32[3,8,896]{2,1,0:T(8,128)S(1)}, u32[]{:S(2)}, u32[]{:S(2)}) %collective-permute-start.3) | collective-permute-done | bytes 86048 | tf_op jit(solution)/shard_map/ppermute | solution.py:29
  52.9 0.1 collective-permute-start.5
  52.9 0.5 collective-permute-start.4
  53.4 1.1 %collective-permute-done.5.second = f32[8,896]{1,0:T(8,128)S(1)} collective-permute-done((f32[8,896]{1,0:T(8,128)S(1)}, f32[8,896]{1,0:T(8,128)S(1)}, u32[]{:S(2)}, u32[]{:S(2)}) %collective-permute-start.5) | collective-permute-done | bytes 28704 | tf_op jit(solution)/shard_map/ppermute | solution.py:29
  54.5 4.5 %collective-permute-done.4.first = f32[8,896]{1,0:T(8,128)S(1)} collective-permute-done((f32[8,896]{1,0:T(8,128)S(1)}, f32[8,896]{1,0:T(8,128)S(1)}, u32[]{:S(2)}, u32[]{:S(2)}) %collective-permute-start.4) | collective-permute-done | bytes 28704 | tf_op jit(solution)/shard_map/ppermute | solution.py:29
  59.0 0.6 %finish.1 = (f32[3,4,128]{2,1,0:T(4,128)}, f32[8,315]{1,0:T(8,128)}) custom-call(f32[3,8,896]{2,1,0:T(8,128)S(1)} %add.3.middle, f32[8,896]{1,0:T(8,128)S(1)} %collective-permute-done.4.first, f32[8,896]{1,0:T(8,128)S(1)} %collective-permute-done.5.second), custom_call_target="tpu_custom_call" | custom-call | tf_op jit(solution)/shard_map/finish/pallas_call | solution.py:382
  (28 shorter events, 0.1 us)
Async XLA Ops:
  0.6 18.7 %copy-start.13 = (s32[1,1,32]{2,1,0:T(1,128)S(1)}, s32[1,1,32]{2,1,0:T(1,128)}, u32[]{:S(2)}) copy-start(s32[1,1,32]{2,1,0:T(1,128)} %param.18) | copy-start | bytes 388
  0.6 18.7 %copy-start.12 = (s32[1,1,32,12]{2,1,3,0:T(1,128)S(1)}, s32[1,1,32,12]{2,1,3,0:T(1,128)}, u32[]{:S(2)}) copy-start(s32[1,1,32,12]{2,1,3,0:T(1,128)} %param.17) | copy-start | bytes 4612
  0.7 0.8 %copy-start = (f32[1,1,3,4096]{3,1,2,0:T(1,128)S(1)}, f32[1,1,3,4096]{3,1,2,0:T(1,128)}, u32[]{:S(2)}) copy-start(f32[1,1,3,4096]{3,1,2,0:T(1,128)} %param.10) | copy-start | bytes 147460
  1.5 0.8 %copy-start.2 = (f32[1,1,3,4096]{3,1,2,0:T(1,128)S(1)}, f32[1,1,3,4096]{3,1,2,0:T(1,128)}, u32[]{:S(2)}) copy-start(f32[1,1,3,4096]{3,1,2,0:T(1,128)} %param.11) | copy-start | bytes 147460
  2.3 0.8 %copy-start.5 = (f32[1,1,3,4096]{3,1,2,0:T(1,128)S(1)}, f32[1,1,3,4096]{3,1,2,0:T(1,128)}, u32[]{:S(2)}) copy-start(f32[1,1,3,4096]{3,1,2,0:T(1,128)} %param.12) | copy-start | bytes 147460
  3.1 0.7 %copy-start.8 = (s32[1,1,8,2]{2,3,1,0:T(2,128)S(1)}, s32[1,1,8,2]{2,3,1,0:T(2,128)}, u32[]{:S(2)}) copy-start(s32[1,1,8,2]{2,3,1,0:T(2,128)} %param.15) | copy-start | bytes 196
  3.7 0.7 %copy-start.9 = (s32[1,1,8]{2,1,0:T(1,128)S(1)}, s32[1,1,8]{2,1,0:T(1,128)}, u32[]{:S(2)}) copy-start(s32[1,1,8]{2,1,0:T(1,128)} %param.16) | copy-start | bytes 100
  4.4 14.9 %copy-start.1 = (f32[1,1,3,4096]{3,1,2,0:T(1,128)S(1)}, f32[1,1,3,4096]{3,1,2,0:T(1,128)}, u32[]{:S(2)}) copy-start(f32[1,1,3,4096]{3,1,2,0:T(1,128)} %param.10) | copy-start | bytes 147460
  5.0 9.7 %collective-permute-start = (f32[12,8,128]{2,1,0:T(8,128)S(1)}, f32[12,8,128]{2,1,0:T(8,128)S(1)}, u32[]{:S(2)}, u32[]{:S(2)}) collective-permute-start(f32[12,8,128]{2,1,0:T(8,128)S(1)} %get-tuple-element.13), channel_id=1, source_target_pairs={{16,0},{0,16},{17,1},{1,17},{18,2},{2,18},{19,3},{3,19},{20,4},{4,... | collective-permute-start | bytes 147464 | tf_op jit(solution)/shard_map/ppermute | solution.py:29
  8.1 0.8 %copy-start.3 = (f32[1,1,3,4096]{3,1,2,0:T(1,128)S(1)}, f32[1,1,3,4096]{3,1,2,0:T(1,128)}, u32[]{:S(2)}) copy-start(f32[1,1,3,4096]{3,1,2,0:T(1,128)} %param.11) | copy-start | bytes 147460
  8.9 0.8 %copy-start.6 = (f32[1,1,3,4096]{3,1,2,0:T(1,128)S(1)}, f32[1,1,3,4096]{3,1,2,0:T(1,128)}, u32[]{:S(2)}) copy-start(f32[1,1,3,4096]{3,1,2,0:T(1,128)} %param.12) | copy-start | bytes 147460
  9.7 0.7 %copy-start.11 = (s32[1,1,4096]{2,1,0:T(1,128)S(1)}, s32[1,1,4096]{2,1,0:T(1,128)}, u32[]{:S(2)}) copy-start(s32[1,1,4096]{2,1,0:T(1,128)} %param.13) | copy-start | bytes 49156
  10.4 0.8 %copy-start.14 = (f32[3,40,128]{2,1,0:T(8,128)S(1)}, f32[3,40,128]{2,1,0:T(8,128)}, u32[]{:S(2)}) copy-start(f32[3,40,128]{2,1,0:T(8,128)} %constant.2.clone.exponents) | copy-start | bytes 184324
  14.7 9.9 %copy-start.4 = (f32[1,1,3,4096]{3,1,2,0:T(1,128)S(1)}, f32[1,1,3,4096]{3,1,2,0:T(1,128)}, u32[]{:S(2)}) copy-start(f32[1,1,3,4096]{3,1,2,0:T(1,128)} %param.11) | copy-start | bytes 147460
  14.8 9.9 %copy-start.7 = (f32[1,1,3,4096]{3,1,2,0:T(1,128)S(1)}, f32[1,1,3,4096]{3,1,2,0:T(1,128)}, u32[]{:S(2)}) copy-start(f32[1,1,3,4096]{3,1,2,0:T(1,128)} %param.12) | copy-start | bytes 147460
  14.8 9.9 %copy-start.10 = (s32[1,1,2,4096]{3,2,1,0:T(2,128)S(1)}, s32[1,1,2,4096]{3,2,1,0:T(2,128)}, u32[]{:S(2)}) copy-start(s32[1,1,2,4096]{3,2,1,0:T(2,128)} %param.14) | copy-start | bytes 98308
  14.8 9.8 %collective-permute-start.1 = (f32[6,8,128]{2,1,0:T(8,128)S(1)}, f32[6,8,128]{2,1,0:T(8,128)S(1)}, u32[]{:S(2)}, u32[]{:S(2)}) collective-permute-start(f32[6,8,128]{2,1,0:T(8,128)S(1)} %pad_maximum_fusion), channel_id=1, source_target_pairs={{15,0},{0,1},{1,2},{2,3},{3,4},{4,5},{5,6},{6,7},{7,8},{8,9},{9,10... | collective-permute-start | bytes 73736 | tf_op jit(solution)/shard_map/ppermute | solution.py:29
  14.9 9.7 %collective-permute-start.2 = (f32[6,8,128]{2,1,0:T(8,128)S(1)}, f32[6,8,128]{2,1,0:T(8,128)S(1)}, u32[]{:S(2)}, u32[]{:S(2)}) collective-permute-start(f32[6,8,128]{2,1,0:T(8,128)S(1)} %pad_maximum_fusion.1), channel_id=1, source_target_pairs={{1,0},{2,1},{3,2},{4,3},{5,4},{6,5},{7,6},{8,7},{9,8},{10,9},{11,1... | collective-permute-start | bytes 73736 | tf_op jit(solution)/shard_map/ppermute | solution.py:29
  48.3 4.6 %collective-permute-start.3 = (f32[3,8,896]{2,1,0:T(8,128)S(1)}, f32[3,8,896]{2,1,0:T(8,128)S(1)}, u32[]{:S(2)}, u32[]{:S(2)}) collective-permute-start(f32[3,8,896]{2,1,0:T(8,128)S(1)} %get-tuple-element.17), channel_id=1, source_target_pairs={{16,0},{0,16},{17,1},{1,17},{18,2},{2,18},{19,3},{3,19},{20,4},{4,... | collective-permute-start | bytes 258056 | tf_op jit(solution)/shard_map/ppermute | solution.py:29
  52.9 1.6 %collective-permute-start.5 = (f32[8,896]{1,0:T(8,128)S(1)}, f32[8,896]{1,0:T(8,128)S(1)}, u32[]{:S(2)}, u32[]{:S(2)}) collective-permute-start(f32[8,896]{1,0:T(8,128)S(1)} %get-tuple-element.24), channel_id=1, source_target_pairs={{1,0},{2,1},{3,2},{4,3},{5,4},{6,5},{7,6},{8,7},{9,8},{10,9},{11,1... | collective-permute-start | bytes 86024 | tf_op jit(solution)/shard_map/ppermute | solution.py:29
  52.9 6.0 %collective-permute-start.4 = (f32[8,896]{1,0:T(8,128)S(1)}, f32[8,896]{1,0:T(8,128)S(1)}, u32[]{:S(2)}, u32[]{:S(2)}) collective-permute-start(f32[8,896]{1,0:T(8,128)S(1)} %get-tuple-element.25), channel_id=1, source_target_pairs={{15,0},{0,1},{1,2},{2,3},{3,4},{4,5},{5,6},{6,7},{7,8},{8,9},{9,10... | collective-permute-start | bytes 86024 | tf_op jit(solution)/shard_map/ppermute | solution.py:29

commit v3 on v2

--- a/solution.py
+++ b/solution.py
@@ -23,10 +23,25 @@
 bf16 = jnp.bfloat16
 
 
-def passed_along(block, axis, distance):
-    size = lax.axis_size(axis)
-    route = [((i - distance) % size, i) for i in range(size)]
-    return lax.ppermute(block, axis, route)
+def moved(block, offset):
+    width, length = lax.axis_size("dx"), lax.axis_size("dy")
+    route = []
+    for i in range(width):
+        for j in range(length):
+            target = (i + offset[0]) % width * length + (j + offset[1]) % length
+            route.append((i * length + j, target))
+    return lax.ppermute(block, ("dx", "dy"), route)
+
+
+def packet_plan(merged):
+    if merged:
+        return [((1, 1), (2, 7)), ((1, -1), (0, 5)), ((1, 0), (1, 6)), ((0, 1), (4,)), ((0, -1), (3,))]
+    return [(neighbour_offsets[k], (k,)) for k in range(8)]
+
+
+def owner_plan(merged):
+    plan = [(offset, tuple(k + (k > 3) for k in held)) for offset, held in packet_plan(merged)]
+    return [((0, 0), (4,))] + plan
 
 
 def exponent_table():
@@ -53,21 +68,27 @@
     return [b[1] * l[2] - b[2] * l[1], b[2] * l[0] - b[0] * l[2], b[0] * l[1] - b[1] * l[0]]
 
 
-def pack_kernel(ghost_list, ghost_count, mid, line, burgers, out_x, out_up, out_down):
-    slots = ghost_list.shape[0]
-    for k in range(8):
-        for g in range(slots):
-            valid = jnp.where(g < ghost_count[0, k], 1.0, 0.0).astype(f32)
-            at = pl.ds(ghost_list[g, k], 1)
-            rows = [mid[c, at] - 0.5 for c in range(3)]
-            rows += cross([burgers[c, at] for c in range(3)], [line[c, at] for c in range(3)])
-            packet = jnp.concatenate(rows + [jnp.zeros((2, TILE), f32)], axis=0) * valid
-            if k == 3:
-                out_down[g] = packet
-            elif k == 4:
-                out_up[g] = packet
-            else:
-                out_x[(k if k < 3 else k - 2) * slots + g] = packet
+def pack_kernel(plan, *refs):
+    (ghost_list, ghost_count), arrays = refs[:2], refs[2:10]
+    packets, copies, (lists, counts, sems) = refs[10:-11], refs[-11:-3], refs[-3:]
+    started = [pltpu.make_async_copy(ghost_list, lists, sems.at[8])]
+    started += [pltpu.make_async_copy(ghost_count, counts, sems.at[9])]
+    started += [pltpu.make_async_copy(a, b, sems.at[k]) for k, (a, b) in enumerate(zip(arrays, copies))]
+    for copy in started:
+        copy.start()
+    for copy in started:
+        copy.wait()
+    mid, line, burgers = copies[:3]
+    slots = lists.shape[0]
+    for out, (offset, held) in zip(packets, plan):
+        for place, k in enumerate(held):
+            for g in range(slots):
+                valid = jnp.where(g < counts[0, k], 1.0, 0.0).astype(f32)
+                at = pl.ds(lists[g, k], 1)
+                rows = [mid[c, at] - 0.5 for c in range(3)]
+                rows += cross([burgers[c, at] for c in range(3)], [line[c, at] for c in range(3)])
+                packet = jnp.concatenate(rows + [jnp.zeros((2, TILE), f32)], axis=0) * valid
+                out[place * slots + g] = packet
 
 
 def moment_kernel(exponents, cell, mid, line, burgers, out, total):
@@ -202,10 +223,12 @@
     ]
 
 
-def pair_kernel(merged, *refs):
-    item_list, spread, mid, line, burgers, x_in, below, above, node, moments = refs[:10]
-    outs, (items, source, features, acc, force, grid) = refs[10:-6], refs[-6:]
-    tiles, slots = mid.shape[1], x_in.shape[0] // 6
+def pair_kernel(merged, slots, *refs):
+    item_list, spread, mid, line, burgers, node, moments = refs[:7]
+    plan, owners = packet_plan(merged), owner_plan(merged)
+    arrivals, outs = refs[7 : 7 + len(plan)], refs[7 + len(plan) : -6]
+    items, source, features, acc, force, grid = refs[-6:]
+    tiles = mid.shape[1]
     pool = tiles + 8 * slots
     total = item_list[0]
 
@@ -224,8 +247,9 @@
         source[c + 3, 0:tiles] = product[c]
     for c in range(6):
         source[c, pool : pool + 1] = jnp.zeros((1, TILE), f32)
-    groups = [(below, 1), (x_in, 4), (above, 1), (below, 0), (above, 0), (below, 2), (x_in, 1), (above, 2)]
-    for q, (arrived, place) in enumerate(groups):
+    where = {k: (arrived, place) for arrived, (offset, held) in zip(arrivals, plan) for place, k in enumerate(held)}
+    for q in range(8):
+        arrived, place = where[7 - q]
         shift = neighbour_offsets[q] + (0,) * 4
         for g in range(slots):
             at = tiles + q * slots + g
@@ -290,18 +314,18 @@
             blocks.append(jnp.concatenate([sums[c][k : k + 1] for c in range(3)] + [jnp.zeros((5, NODE_LOW), f32)], axis=0))
         return jnp.concatenate([moments[d]] + blocks, axis=1)
 
-    for b in range(3):
-        low, middle, high = part(b), part(3 + b), part(6 + b)
-        outs[0][b] = middle
-        if merged:
-            outs[1][b] = low + high
-        else:
-            outs[1][b] = high
-            outs[2][b] = low
-
-
-def finish_kernel(middle, first, second, node_force, cells):
-    total = middle[1] + first[...] + second[...]
+    for out, (offset, held) in zip(outs, owners):
+        value = part(held[0])
+        for d in held[1:]:
+            value = value + part(d)
+        out[...] = value
+
+
+def finish_kernel(*refs):
+    parts, (node_force, cells) = refs[:-2], refs[-2:]
+    total = parts[0][...]
+    for other in parts[1:]:
+        total = total + other[...]
     cells[...] = total[:, : cells.shape[1]]
     for k in range(NODE_DEV // TILE):
         at = MOMENT_LANES + k * TILE
@@ -312,58 +336,62 @@
     tiles, slots = seg_mid.shape[-1] // TILE, ghost_list.shape[-1]
     mid, line, burgers = [v.reshape(3, tiles, TILE) for v in (seg_mid, seg_line, seg_burgers)]
     cell = seg_cell.reshape(tiles, TILE)
+    exponents = jnp.asarray(exponent_table())
+    inputs = (mid, line, burgers, cell, seg_node[0, 0], exponents)
+    inputs += (pair_list[0].transpose(2, 0, 1), pair_count[0])
     pairs = pair_list.shape[-1]
     plain = pl.BlockSpec()
     vmem = pl.BlockSpec(memory_space=pltpu.VMEM)
+    hbm = pl.BlockSpec(memory_space=pltpu.HBM)
     smem = pl.BlockSpec(memory_space=pltpu.SMEM)
     shape = jax.ShapeDtypeStruct
     params = pltpu.CompilerParams(vmem_limit_bytes=32 * 2**20)
     cost = lambda flops: pl.CostEstimate(flops=flops, transcendentals=0, bytes_accessed=0)
-    out_x, out_up, out_down = pl.pallas_call(
-        pack_kernel,
-        in_specs=[smem, smem] + [plain] * 3,
-        out_specs=[plain] * 3,
-        out_shape=[shape((k, 8, TILE), f32) for k in (6 * slots, slots, slots)],
+    plan, owners = packet_plan(merged), owner_plan(merged)
+    lists, counts = ghost_list[0, 0].T, ghost_count[0]
+    results = pl.pallas_call(
+        functools.partial(pack_kernel, plan),
+        in_specs=[hbm] * 10,
+        out_specs=[vmem] * (len(plan) + 8),
+        out_shape=[shape((len(held) * slots, 8, TILE), f32) for offset, held in plan]
+        + [shape(v.shape, v.dtype) for v in inputs],
+        scratch_shapes=[
+            pltpu.SMEM(lists.shape, jnp.int32),
+            pltpu.SMEM(counts.shape, jnp.int32),
+            pltpu.SemaphoreType.DMA((10,)),
+        ],
         compiler_params=params,
         name="pack",
-    )(ghost_list[0, 0].T, ghost_count[0], mid, line, burgers)
-    if merged:
-        x_in = passed_along(out_x, "dx", 1)
-    else:
-        x_in = jnp.concatenate(
-            [passed_along(out_x[: 3 * slots], "dx", -1), passed_along(out_x[3 * slots :], "dx", 1)]
-        )
-    pick = lambda k: x_in[k * slots : (k + 1) * slots]
-    below = passed_along(jnp.concatenate([out_up, pick(5), pick(2)]), "dy", 1)
-    above = passed_along(jnp.concatenate([out_down, pick(3), pick(0)]), "dy", -1)
+    )(*[pltpu.with_memory_space_constraint(v, pltpu.HBM) for v in (lists, counts, *inputs)])
+    arrivals = [moved(packet, offset) for packet, (offset, held) in zip(results, plan)]
+    mid, line, burgers, cell, node, exponents, pair_rows, pair_limits = results[len(plan) :]
     moments = pl.pallas_call(
         moment_kernel,
-        in_specs=[plain] * 5,
-        out_specs=plain,
+        in_specs=[vmem] * 5,
+        out_specs=vmem,
         out_shape=shape((9, CELL_DEV, MOMENT_LANES), f32),
         scratch_shapes=[pltpu.VMEM((736, TILE), f32)],
         compiler_params=params,
         cost_estimate=cost(3 * 10**9),
         name="moments",
-    )(jnp.asarray(exponent_table()), cell, mid, line, burgers)
+    )(exponents, cell, mid, line, burgers)
     room = tiles * pairs + 16
     item_list, spread = pl.pallas_call(
         prepare_kernel,
-        in_specs=[smem, smem, plain],
+        in_specs=[smem, smem, vmem],
         out_specs=[smem, vmem],
         out_shape=[shape((room,), jnp.int32), shape((tiles, 3, TILE, TILE), f32)],
         compiler_params=params,
         cost_estimate=cost(3 * 10**9),
         name="prepare",
-    )(pair_list[0].transpose(2, 0, 1), pair_count[0], mid)
+    )(pair_rows, pair_limits, mid)
     width = MOMENT_LANES + NODE_DEV
-    count = 2 if merged else 3
     pool = tiles + 8 * slots
     parts = pl.pallas_call(
-        functools.partial(pair_kernel, merged),
-        in_specs=[smem, vmem] + [plain] * 8,
-        out_specs=[plain] * count,
-        out_shape=[shape((3, 8, width), f32)] * count,
+        functools.partial(pair_kernel, merged, slots),
+        in_specs=[smem] + [vmem] * (6 + len(plan)),
+        out_specs=[vmem] * len(owners),
+        out_shape=[shape((8, width), f32)] * len(owners),
         scratch_shapes=[
             pltpu.SMEM((room,), jnp.int32),
             pltpu.VMEM((6, pool + 1, TILE), f32),
@@ -375,18 +403,16 @@
         compiler_params=params,
         cost_estimate=cost(10**10),
         name="pairs",
-    )(item_list, spread, mid, line, burgers, x_in, below, above, seg_node[0, 0], moments)
-    middle = parts[0] + passed_along(parts[1], "dx", 1)
-    if not merged:
-        middle = middle + passed_along(parts[2], "dx", -1)
+    )(item_list, spread, mid, line, burgers, node, moments, *arrivals)
+    totals = [parts[0]] + [moved(v, offset) for v, (offset, held) in zip(parts[1:], owners[1:])]
     node_force, cells = pl.pallas_call(
         finish_kernel,
-        in_specs=[plain] * 3,
+        in_specs=[vmem] * len(totals),
         out_specs=[plain] * 2,
         out_shape=[shape((3, NODE_DEV // TILE, TILE), f32), shape((CELL_DEV, 9 * MONO), f32)],
         compiler_params=params,
         name="finish",
-    )(middle, passed_along(middle[2], "dy", 1), passed_along(middle[0], "dy", -1))
+    )(*totals)
     return node_force.reshape(1, 1, 3, NODE_DEV), cells.T
 
 

time: 59.5 us -> 58 us (0.975)
  starting transfers between devices: 8.14 us -> 22.6 us
  waiting for transfers between devices: 10 us -> 1.57 us
  local copies, waits for them, and re-layouts: 6.92 us -> 0 us
  Pallas kernels: 33.7 us -> 32.9 us
    ppermute x6 -> x10, starting transfers between devices: 8.14 us -> 22.6 us  [moved(): return lax.ppermute(block, ('dx', 'dy'), route)]
    ppermute x6 -> x10, waiting for transfers between devices: 10 us -> 1.57 us  [moved(): return lax.ppermute(block, ('dx', 'dy'), route)]
    unnamed x30 -> x0, local copies, waits for them, and re-layouts: 6.9 us -> none
    pallas_call x5, Pallas kernels: 33.7 us -> 32.9 us  [the longest x1 22.3 us: on_device(): pl.pallas_call(functools.partial(pair_kernel, merged, slots), in_specs=[s...]
  transfers between devices with their start and end apart: 6 -> 10, of which waited for: 3 -> 1; matrix products, arithmetic and copies ran while one was open for 0% -> 0% of each run, Pallas kernels for 15% -> 15%
where the time goes in v3:
time: 58 us; the launch traced here: 57.8 us
  Pallas kernels  32.9 us (57%)
  starting transfers between devices  22.6 us (39%)
  waiting for transfers between devices  1.57 us (3%)
  between operations  0.72 us (1%)
    ppermute x10, starting transfers between devices, moved(): return lax.ppermute(block, ('dx', 'dy'), route)  22.6 us
    pallas_call x1, Pallas kernels, on_device(): pl.pallas_call(functools.partial(pair_kernel, merged, slots), in_specs=[s...  22.3 us
    pallas_call x1, Pallas kernels, on_device(): pl.pallas_call(prepare_kernel, in_specs=[smem, smem, vmem], out_specs=[sm...  5.25 us
    pallas_call x1, Pallas kernels, on_device(): pl.pallas_call(moment_kernel, in_specs=[vmem] * 5, out_specs=vmem, out_sh...  3.52 us
    ppermute x10, waiting for transfers between devices, moved(): return lax.ppermute(block, ('dx', 'dy'), route)  1.57 us
  transfers between devices with their start and end apart: 10, of which 1 were waited for; matrix products, arithmetic and copies ran while one was open for 0% of the time, Pallas kernels for 15%

profile of v3, /device:TPU:0, one launch (start us, length us, event | category | flops | bytes accessed | tf_op | source)
XLA Modules:
  0.0 57.8 jit_solution(1706483501745293708)
XLA Ops:
  0.6 1.1 %pack.1 = (f32[4,8,128]{2,1,0:T(8,128)S(1)}, f32[4,8,128]{2,1,0:T(8,128)S(1)}, f32[4,8,128]{2,1,0:T(8,128)S(1)}, f32[2,8,128]{2,1,0:T(8,128)S(1)}, f32[2,8,128]{...) custom-call(s32[2,8]{1,0:T(2,128)} %bitcast.21, ...), custom_call_target="tpu_custom_call" | custom-call | tf_op jit(solution)/shard_map/pack/pallas_call | solution.py:352
  1.8 0.5 collective-permute-start.3
  2.3 5.0 %collective-permute-start.4 = (f32[2,8,128]{2,1,0:T(8,128)S(1)}, f32[2,8,128]{2,1,0:T(8,128)S(1)}, u32[]{:S(2)}, u32[]{:S(2)}) collective-permute-start(f32[2,8,128]{2,1,0:T(8,128)S(1)} %get-tuple-element.39), channel_id=1, source_target_pairs={{0,15},{1,0},{2,1},{3,2},{4,3},{5,4},{6,5},{7,6},{8,7},{9,8},{10,9... | collective-permute-start | bytes 24584 | tf_op jit(solution)/shard_map/ppermute | solution.py:33
  7.4 0.0 collective-permute-start
  7.4 5.3 %collective-permute-start.1 = (f32[4,8,128]{2,1,0:T(8,128)S(1)}, f32[4,8,128]{2,1,0:T(8,128)S(1)}, u32[]{:S(2)}, u32[]{:S(2)}) collective-permute-start(f32[4,8,128]{2,1,0:T(8,128)S(1)} %get-tuple-element.36), channel_id=1, source_target_pairs={{0,31},{1,16},{2,17},{3,18},{4,19},{5,20},{6,21},{7,22},{8,23},{9,... | collective-permute-start | bytes 49160 | tf_op jit(solution)/shard_map/ppermute | solution.py:33
  12.7 1.9 %collective-permute-start.2 = (f32[4,8,128]{2,1,0:T(8,128)S(1)}, f32[4,8,128]{2,1,0:T(8,128)S(1)}, u32[]{:S(2)}, u32[]{:S(2)}) collective-permute-start(f32[4,8,128]{2,1,0:T(8,128)S(1)} %get-tuple-element.37), channel_id=1, source_target_pairs={{0,16},{1,17},{2,18},{3,19},{4,20},{5,21},{6,22},{7,23},{8,24},{9,... | collective-permute-start | bytes 49160 | tf_op jit(solution)/shard_map/ppermute | solution.py:33
  14.6 5.2 %prepare.1 = (s32[400]{0:T(512)S(1)}, f32[32,3,128,128]{3,2,1,0:T(8,128)S(1)}) custom-call(s32[12,1,32]{2,1,0:T(1,128)S(1)} %get-tuple-element.25.pair_list, s32[1,32]{1,0:T(1,128)S(1)} %get-tuple-element.26.pair_count, f32[3,32,128]{2,1,0:T(8,128)S(1)} %get-tuple-element.27.mid.refs_2_), custom_call_target="tpu_custom_call" | custom-call | flops 3000000000 | tf_op jit(solution)/shard_map/prepare/pallas_call | solution.py:379
  19.8 3.5 %moments.1.refs_6_ = f32[9,8,384]{2,1,0:T(8,128)S(1)} custom-call(f32[3,40,128]{2,1,0:T(8,128)S(1)} %get-tuple-element.33.exponents, s32[32,128]{1,0:T(8,128)S(1)} %get-tuple-element.34.cell, f32[3,32,128]{2,1,0:T(8,128)S(1)} %get-tuple-element.27.mid.refs_2_, f32[3,32,128]{2,1,0:T(8,128)S(1)} %get-tuple-element.30.line.refs_3_, ...), custom_call_target="tpu_custom_call" | custom-call | flops 3000000000 | tf_op jit(solution)/shard_map/moments/pallas_call | solution.py:368
  23.4 0.0 collective-permute-done.3.refs_10_
  23.4 0.0 collective-permute-done.4.refs_11_
  23.4 0.0 collective-permute-done.refs_7_
  23.4 0.0 collective-permute-done.1.refs_8_
  23.4 0.0 collective-permute-done.2.refs_9_
  23.4 22.3 %pairs.1 = (f32[8,896]{1,0:T(8,128)S(1)}, f32[8,896]{1,0:T(8,128)S(1)}, f32[8,896]{1,0:T(8,128)S(1)}, f32[8,896]{1,0:T(8,128)S(1)}, f32[8,896]{1,0:T(8,128)S(1)}, /*index=5*/f32[8,896]{1,0:T(8,128)S(1)}) custom-call(s32[400]{0:T(512)S(1)} %get-tuple-element.28.refs_0_, f32[32,3,128,128]{3,2,1,0:T(8,128)S(1)} %get-tuple-element.29.refs_1_, ...), custom_call_target="tpu_custom_call" | custom-call | flops 10000000000 | tf_op jit(solution)/shard_map/pairs/pallas_call | solution.py:390
  45.8 0.1 collective-permute-start.5
  45.8 5.3 %collective-permute-start.6 = (f32[8,896]{1,0:T(8,128)S(1)}, f32[8,896]{1,0:T(8,128)S(1)}, u32[]{:S(2)}, u32[]{:S(2)}) collective-permute-start(f32[8,896]{1,0:T(8,128)S(1)} %get-tuple-element.42), channel_id=1, source_target_pairs={{0,31},{1,16},{2,17},{3,18},{4,19},{5,20},{6,21},{7,22},{8,23},{9,... | collective-permute-start | bytes 86024 | tf_op jit(solution)/shard_map/ppermute | solution.py:33
  51.2 0.0 collective-permute-start.7
  51.2 0.0 collective-permute-start.8
  51.2 4.4 %collective-permute-start.9 = (f32[8,896]{1,0:T(8,128)S(1)}, f32[8,896]{1,0:T(8,128)S(1)}, u32[]{:S(2)}, u32[]{:S(2)}) collective-permute-start(f32[8,896]{1,0:T(8,128)S(1)} %get-tuple-element.45), channel_id=1, source_target_pairs={{0,15},{1,0},{2,1},{3,2},{4,3},{5,4},{6,5},{7,6},{8,7},{9,8},{10,9... | collective-permute-start | bytes 86024 | tf_op jit(solution)/shard_map/ppermute | solution.py:33
  55.6 0.0 collective-permute-done.5.refs_1_
  55.6 0.0 collective-permute-done.6.refs_2_
  55.6 1.5 %collective-permute-done.8.refs_4_ = f32[8,896]{1,0:T(8,128)S(1)} collective-permute-done((f32[8,896]{1,0:T(8,128)S(1)}, f32[8,896]{1,0:T(8,128)S(1)}, u32[]{:S(2)}, u32[]{:S(2)}) %collective-permute-start.8) | collective-permute-done | bytes 28704 | tf_op jit(solution)/shard_map/ppermute | solution.py:33
  57.1 0.0 collective-permute-done.9.refs_5_
  57.2 0.6 %finish.1 = (f32[3,4,128]{2,1,0:T(4,128)}, f32[8,315]{1,0:T(8,128)}) custom-call(f32[8,896]{1,0:T(8,128)S(1)} %get-tuple-element.40.refs_0_, f32[8,896]{1,0:T(8,128)S(1)} %collective-permute-done.5.refs_1_, f32[8,896]{1,0:T(8,128)S(1)} %collective-permute-done.6.refs_2_, f32[8,896]{1,0:T(8,128)S(1)} %collective-permute-done.7.refs_3_, ...), custom_call_target="tpu_custom_call" | custom-call | tf_op jit(solution)/shard_map/finish/pallas_call | solution.py:408
  (1 shorter events, 0.0 us)
Async XLA Ops:
  1.8 21.6 %collective-permute-start.3 = (f32[2,8,128]{2,1,0:T(8,128)S(1)}, f32[2,8,128]{2,1,0:T(8,128)S(1)}, u32[]{:S(2)}, u32[]{:S(2)}) collective-permute-start(f32[2,8,128]{2,1,0:T(8,128)S(1)} %get-tuple-element.38), channel_id=1, source_target_pairs={{0,1},{1,2},{2,3},{3,4},{4,5},{5,6},{6,7},{7,8},{8,9},{9,10},{10,1... | collective-permute-start | bytes 24584 | tf_op jit(solution)/shard_map/ppermute | solution.py:33
  2.3 21.1 %collective-permute-start.4 = (f32[2,8,128]{2,1,0:T(8,128)S(1)}, f32[2,8,128]{2,1,0:T(8,128)S(1)}, u32[]{:S(2)}, u32[]{:S(2)}) collective-permute-start(f32[2,8,128]{2,1,0:T(8,128)S(1)} %get-tuple-element.39), channel_id=1, source_target_pairs={{0,15},{1,0},{2,1},{3,2},{4,3},{5,4},{6,5},{7,6},{8,7},{9,8},{10,9... | collective-permute-start | bytes 24584 | tf_op jit(solution)/shard_map/ppermute | solution.py:33
  7.4 16.0 %collective-permute-start = (f32[4,8,128]{2,1,0:T(8,128)S(1)}, f32[4,8,128]{2,1,0:T(8,128)S(1)}, u32[]{:S(2)}, u32[]{:S(2)}) collective-permute-start(f32[4,8,128]{2,1,0:T(8,128)S(1)} %get-tuple-element.35), channel_id=1, source_target_pairs={{0,17},{1,18},{2,19},{3,20},{4,21},{5,22},{6,23},{7,24},{8,25},{9,... | collective-permute-start | bytes 49160 | tf_op jit(solution)/shard_map/ppermute | solution.py:33
  7.4 16.0 %collective-permute-start.1 = (f32[4,8,128]{2,1,0:T(8,128)S(1)}, f32[4,8,128]{2,1,0:T(8,128)S(1)}, u32[]{:S(2)}, u32[]{:S(2)}) collective-permute-start(f32[4,8,128]{2,1,0:T(8,128)S(1)} %get-tuple-element.36), channel_id=1, source_target_pairs={{0,31},{1,16},{2,17},{3,18},{4,19},{5,20},{6,21},{7,22},{8,23},{9,... | collective-permute-start | bytes 49160 | tf_op jit(solution)/shard_map/ppermute | solution.py:33
  12.7 10.7 %collective-permute-start.2 = (f32[4,8,128]{2,1,0:T(8,128)S(1)}, f32[4,8,128]{2,1,0:T(8,128)S(1)}, u32[]{:S(2)}, u32[]{:S(2)}) collective-permute-start(f32[4,8,128]{2,1,0:T(8,128)S(1)} %get-tuple-element.37), channel_id=1, source_target_pairs={{0,16},{1,17},{2,18},{3,19},{4,20},{5,21},{6,22},{7,23},{8,24},{9,... | collective-permute-start | bytes 49160 | tf_op jit(solution)/shard_map/ppermute | solution.py:33
  45.8 9.8 %collective-permute-start.5 = (f32[8,896]{1,0:T(8,128)S(1)}, f32[8,896]{1,0:T(8,128)S(1)}, u32[]{:S(2)}, u32[]{:S(2)}) collective-permute-start(f32[8,896]{1,0:T(8,128)S(1)} %get-tuple-element.41), channel_id=1, source_target_pairs={{0,17},{1,18},{2,19},{3,20},{4,21},{5,22},{6,23},{7,24},{8,25},{9,... | collective-permute-start | bytes 86024 | tf_op jit(solution)/shard_map/ppermute | solution.py:33
  45.8 9.8 %collective-permute-start.6 = (f32[8,896]{1,0:T(8,128)S(1)}, f32[8,896]{1,0:T(8,128)S(1)}, u32[]{:S(2)}, u32[]{:S(2)}) collective-permute-start(f32[8,896]{1,0:T(8,128)S(1)} %get-tuple-element.42), channel_id=1, source_target_pairs={{0,31},{1,16},{2,17},{3,18},{4,19},{5,20},{6,21},{7,22},{8,23},{9,... | collective-permute-start | bytes 86024 | tf_op jit(solution)/shard_map/ppermute | solution.py:33
  51.2 4.5 %collective-permute-start.7 = (f32[8,896]{1,0:T(8,128)S(1)}, f32[8,896]{1,0:T(8,128)S(1)}, u32[]{:S(2)}, u32[]{:S(2)}) collective-permute-start(f32[8,896]{1,0:T(8,128)S(1)} %get-tuple-element.43), channel_id=1, source_target_pairs={{0,16},{1,17},{2,18},{3,19},{4,20},{5,21},{6,22},{7,23},{8,24},{9,... | collective-permute-start | bytes 86024 | tf_op jit(solution)/shard_map/ppermute | solution.py:33
  51.2 6.0 %collective-permute-start.8 = (f32[8,896]{1,0:T(8,128)S(1)}, f32[8,896]{1,0:T(8,128)S(1)}, u32[]{:S(2)}, u32[]{:S(2)}) collective-permute-start(f32[8,896]{1,0:T(8,128)S(1)} %get-tuple-element.44), channel_id=1, source_target_pairs={{0,1},{1,2},{2,3},{3,4},{4,5},{5,6},{6,7},{7,8},{8,9},{9,10},{10,1... | collective-permute-start | bytes 86024 | tf_op jit(solution)/shard_map/ppermute | solution.py:33
  51.2 6.0 %collective-permute-start.9 = (f32[8,896]{1,0:T(8,128)S(1)}, f32[8,896]{1,0:T(8,128)S(1)}, u32[]{:S(2)}, u32[]{:S(2)}) collective-permute-start(f32[8,896]{1,0:T(8,128)S(1)} %get-tuple-element.45), channel_id=1, source_target_pairs={{0,15},{1,0},{2,1},{3,2},{4,3},{5,4},{6,5},{7,6},{8,7},{9,8},{10,9... | collective-permute-start | bytes 86024 | tf_op jit(solution)/shard_map/ppermute | solution.py:33

commit v4 on v2

--- a/solution.py
+++ b/solution.py
@@ -29,6 +29,9 @@
     return lax.ppermute(block, axis, route)
 
 
+PLAN = ((0, 1, 2, 5, 6, 7), (4,), (3,))
+
+
 def exponent_table():
     rows = []
     for degree in range(5):
@@ -53,21 +56,27 @@
     return [b[1] * l[2] - b[2] * l[1], b[2] * l[0] - b[0] * l[2], b[0] * l[1] - b[1] * l[0]]
 
 
-def pack_kernel(ghost_list, ghost_count, mid, line, burgers, out_x, out_up, out_down):
-    slots = ghost_list.shape[0]
-    for k in range(8):
-        for g in range(slots):
-            valid = jnp.where(g < ghost_count[0, k], 1.0, 0.0).astype(f32)
-            at = pl.ds(ghost_list[g, k], 1)
-            rows = [mid[c, at] - 0.5 for c in range(3)]
-            rows += cross([burgers[c, at] for c in range(3)], [line[c, at] for c in range(3)])
-            packet = jnp.concatenate(rows + [jnp.zeros((2, TILE), f32)], axis=0) * valid
-            if k == 3:
-                out_down[g] = packet
-            elif k == 4:
-                out_up[g] = packet
-            else:
-                out_x[(k if k < 3 else k - 2) * slots + g] = packet
+def pack_kernel(*refs):
+    (ghost_list, ghost_count), arrays = refs[:2], refs[2:10]
+    packets, copies, (lists, counts, sems) = refs[10:-11], refs[-11:-3], refs[-3:]
+    started = [pltpu.make_async_copy(ghost_list, lists, sems.at[8])]
+    started += [pltpu.make_async_copy(ghost_count, counts, sems.at[9])]
+    started += [pltpu.make_async_copy(a, b, sems.at[k]) for k, (a, b) in enumerate(zip(arrays, copies))]
+    for copy in started:
+        copy.start()
+    for copy in started:
+        copy.wait()
+    mid, line, burgers = copies[:3]
+    slots = lists.shape[0]
+    for out, held in zip(packets, PLAN):
+        for place, k in enumerate(held):
+            for g in range(slots):
+                valid = jnp.where(g < counts[0, k], 1.0, 0.0).astype(f32)
+                at = pl.ds(lists[g, k], 1)
+                rows = [mid[c, at] - 0.5 for c in range(3)]
+                rows += cross([burgers[c, at] for c in range(3)], [line[c, at] for c in range(3)])
+                packet = jnp.concatenate(rows + [jnp.zeros((2, TILE), f32)], axis=0) * valid
+                out[place * slots + g] = packet
 
 
 def moment_kernel(exponents, cell, mid, line, burgers, out, total):
@@ -202,10 +211,10 @@
     ]
 
 
-def pair_kernel(merged, *refs):
-    item_list, spread, mid, line, burgers, x_in, below, above, node, moments = refs[:10]
+def pair_kernel(merged, slots, *refs):
+    item_list, spread, mid, line, burgers, node, moments, x_in, below, above = refs[:10]
     outs, (items, source, features, acc, force, grid) = refs[10:-6], refs[-6:]
-    tiles, slots = mid.shape[1], x_in.shape[0] // 6
+    tiles = mid.shape[1]
     pool = tiles + 8 * slots
     total = item_list[0]
 
@@ -312,21 +321,34 @@
     tiles, slots = seg_mid.shape[-1] // TILE, ghost_list.shape[-1]
     mid, line, burgers = [v.reshape(3, tiles, TILE) for v in (seg_mid, seg_line, seg_burgers)]
     cell = seg_cell.reshape(tiles, TILE)
+    exponents = jnp.asarray(exponent_table())
+    inputs = (mid, line, burgers, cell, seg_node[0, 0], exponents)
+    inputs += (pair_list[0].transpose(2, 0, 1), pair_count[0])
     pairs = pair_list.shape[-1]
     plain = pl.BlockSpec()
     vmem = pl.BlockSpec(memory_space=pltpu.VMEM)
+    hbm = pl.BlockSpec(memory_space=pltpu.HBM)
     smem = pl.BlockSpec(memory_space=pltpu.SMEM)
     shape = jax.ShapeDtypeStruct
     params = pltpu.CompilerParams(vmem_limit_bytes=32 * 2**20)
     cost = lambda flops: pl.CostEstimate(flops=flops, transcendentals=0, bytes_accessed=0)
-    out_x, out_up, out_down = pl.pallas_call(
+    lists, counts = ghost_list[0, 0].T, ghost_count[0]
+    results = pl.pallas_call(
         pack_kernel,
-        in_specs=[smem, smem] + [plain] * 3,
-        out_specs=[plain] * 3,
-        out_shape=[shape((k, 8, TILE), f32) for k in (6 * slots, slots, slots)],
+        in_specs=[hbm] * 10,
+        out_specs=[vmem] * (len(PLAN) + 8),
+        out_shape=[shape((len(held) * slots, 8, TILE), f32) for held in PLAN]
+        + [shape(v.shape, v.dtype) for v in inputs],
+        scratch_shapes=[
+            pltpu.SMEM(lists.shape, jnp.int32),
+            pltpu.SMEM(counts.shape, jnp.int32),
+            pltpu.SemaphoreType.DMA((10,)),
+        ],
         compiler_params=params,
         name="pack",
-    )(ghost_list[0, 0].T, ghost_count[0], mid, line, burgers)
+    )(*[pltpu.with_memory_space_constraint(v, pltpu.HBM) for v in (lists, counts, *inputs)])
+    out_x, out_up, out_down = results[:3]
+    mid, line, burgers, cell, node, exponents, pair_rows, pair_limits = results[3:]
     if merged:
         x_in = passed_along(out_x, "dx", 1)
     else:
@@ -338,31 +360,31 @@
     above = passed_along(jnp.concatenate([out_down, pick(3), pick(0)]), "dy", -1)
     moments = pl.pallas_call(
         moment_kernel,
-        in_specs=[plain] * 5,
-        out_specs=plain,
+        in_specs=[vmem] * 5,
+        out_specs=vmem,
         out_shape=shape((9, CELL_DEV, MOMENT_LANES), f32),
         scratch_shapes=[pltpu.VMEM((736, TILE), f32)],
         compiler_params=params,
         cost_estimate=cost(3 * 10**9),
         name="moments",
-    )(jnp.asarray(exponent_table()), cell, mid, line, burgers)
+    )(exponents, cell, mid, line, burgers)
     room = tiles * pairs + 16
     item_list, spread = pl.pallas_call(
         prepare_kernel,
-        in_specs=[smem, smem, plain],
+        in_specs=[smem, smem, vmem],
         out_specs=[smem, vmem],
         out_shape=[shape((room,), jnp.int32), shape((tiles, 3, TILE, TILE), f32)],
         compiler_params=params,
         cost_estimate=cost(3 * 10**9),
         name="prepare",
-    )(pair_list[0].transpose(2, 0, 1), pair_count[0], mid)
+    )(pair_rows, pair_limits, mid)
     width = MOMENT_LANES + NODE_DEV
     count = 2 if merged else 3
     pool = tiles + 8 * slots
     parts = pl.pallas_call(
-        functools.partial(pair_kernel, merged),
-        in_specs=[smem, vmem] + [plain] * 8,
-        out_specs=[plain] * count,
+        functools.partial(pair_kernel, merged, slots),
+        in_specs=[smem] + [vmem] * 9,
+        out_specs=[vmem] * count,
         out_shape=[shape((3, 8, width), f32)] * count,
         scratch_shapes=[
             pltpu.SMEM((room,), jnp.int32),
@@ -375,13 +397,13 @@
         compiler_params=params,
         cost_estimate=cost(10**10),
         name="pairs",
-    )(item_list, spread, mid, line, burgers, x_in, below, above, seg_node[0, 0], moments)
+    )(item_list, spread, mid, line, burgers, node, moments, x_in, below, above)
     middle = parts[0] + passed_along(parts[1], "dx", 1)
     if not merged:
         middle = middle + passed_along(parts[2], "dx", -1)
     node_force, cells = pl.pallas_call(
         finish_kernel,
-        in_specs=[plain] * 3,
+        in_specs=[vmem] * 3,
         out_specs=[plain] * 2,
         out_shape=[shape((3, NODE_DEV // TILE, TILE), f32), shape((CELL_DEV, 9 * MONO), f32)],
         compiler_params=params,

time: 59.5 us -> 54.1 us (0.909); the launches traced: 59.6 us -> 53.6 us
  local copies, waits for them, and re-layouts: 6.92 us -> 0.01 us
  starting transfers between devices: 8.14 us -> 9.51 us
  Pallas kernels: 33.7 us -> 32.8 us
    unnamed x30 -> x0, local copies, waits for them, and re-layouts: 6.9 us -> none
    ppermute x6, starting transfers between devices: 8.14 us -> 9.51 us  [passed_along(): return lax.ppermute(block, axis, route)]
    pallas_call x5, Pallas kernels: 33.7 us -> 32.8 us  [the longest x1 22.3 us: on_device(): pl.pallas_call(functools.partial(pair_kernel, merged, slots), in_specs=[s...]
  transfers between devices with their start and end apart: 6 -> 6, of which waited for: 3 -> 3; matrix products, arithmetic and copies ran while one was open for 0% -> 0% of each run, Pallas kernels for 15% -> 16%
where the time goes in v4:
time: 54.1 us; the launch traced here: 53.6 us
  Pallas kernels  32.8 us (61%)
  waiting for transfers between devices  10.5 us (19%)
  starting transfers between devices  9.51 us (18%)
  between operations  0.74 us (1%)
    pallas_call x1, Pallas kernels, on_device(): pl.pallas_call(functools.partial(pair_kernel, merged, slots), in_specs=[s...  22.3 us
    ppermute x6, waiting for transfers between devices, passed_along(): return lax.ppermute(block, axis, route)  10.5 us
    ppermute x6, starting transfers between devices, passed_along(): return lax.ppermute(block, axis, route)  9.51 us
    pallas_call x1, Pallas kernels, on_device(): pl.pallas_call(prepare_kernel, in_specs=[smem, smem, vmem], out_specs=[sm...  5.25 us
    pallas_call x1, Pallas kernels, on_device(): pl.pallas_call(moment_kernel, in_specs=[vmem] * 5, out_specs=vmem, out_sh...  3.52 us
    pallas_call x1, Pallas kernels, on_device(): pl.pallas_call(pack_kernel, in_specs=[hbm] * 10, out_specs=[vmem] * (len(...  1.12 us
  transfers between devices with their start and end apart: 6, of which 3 were waited for; matrix products, arithmetic and copies ran while one was open for 0% of the time, Pallas kernels for 16%

profile of v4, /device:TPU:0, one launch (start us, length us, event | category | flops | bytes accessed | tf_op | source)
XLA Modules:
  0.0 53.6 jit_solution(8712710706876087844)
XLA Ops:
  0.6 1.1 %pack.1 = (f32[12,8,128]{2,1,0:T(8,128)S(1)}, f32[2,8,128]{2,1,0:T(8,128)S(1)}, f32[2,8,128]{2,1,0:T(8,128)S(1)}, f32[3,32,128]{2,1,0:T(8,128)S(1)}, f32[3,32,12...) custom-call(s32[2,8]{1,0:T(2,128)} %bitcast.25, ...), custom_call_target="tpu_custom_call" | custom-call | tf_op jit(solution)/shard_map/pack/pallas_call | solution.py:336
  1.8 3.0 %collective-permute-start = (f32[12,8,128]{2,1,0:T(8,128)S(1)}, f32[12,8,128]{2,1,0:T(8,128)S(1)}, u32[]{:S(2)}, u32[]{:S(2)}) collective-permute-start(f32[12,8,128]{2,1,0:T(8,128)S(1)} %get-tuple-element.29), channel_id=1, source_target_pairs={{16,0},{0,16},{17,1},{1,17},{18,2},{2,18},{19,3},{3,19},{20,4},{4,... | collective-permute-start | bytes 147464 | tf_op jit(solution)/shard_map/ppermute | solution.py:29
  4.8 5.2 %prepare.1 = (s32[400]{0:T(512)S(1)}, f32[32,3,128,128]{3,2,1,0:T(8,128)S(1)}) custom-call(s32[12,1,32]{2,1,0:T(1,128)S(1)} %get-tuple-element.19.pair_list, s32[1,32]{1,0:T(1,128)S(1)} %get-tuple-element.20.pair_count, f32[3,32,128]{2,1,0:T(8,128)S(1)} %get-tuple-element.21.mid.refs_2_), custom_call_target="tpu_custom_call" | custom-call | flops 3000000000 | tf_op jit(solution)/shard_map/prepare/pallas_call | solution.py:372
  10.1 0.0 collective-permute-done.refs_7_
  10.1 0.1 collective-permute-start.1
  10.2 4.4 %collective-permute-start.2 = (f32[6,8,128]{2,1,0:T(8,128)S(1)}, f32[6,8,128]{2,1,0:T(8,128)S(1)}, u32[]{:S(2)}, u32[]{:S(2)}) collective-permute-start(f32[6,8,128]{2,1,0:T(8,128)S(1)} %pad_maximum_fusion.1), channel_id=1, source_target_pairs={{1,0},{2,1},{3,2},{4,3},{5,4},{6,5},{7,6},{8,7},{9,8},{10,9},{11,1... | collective-permute-start | bytes 73736 | tf_op jit(solution)/shard_map/ppermute | solution.py:29
  14.6 3.5 %moments.1.refs_6_ = f32[9,8,384]{2,1,0:T(8,128)S(1)} custom-call(f32[3,40,128]{2,1,0:T(8,128)S(1)} %get-tuple-element.27.exponents, s32[32,128]{1,0:T(8,128)S(1)} %get-tuple-element.28.cell, f32[3,32,128]{2,1,0:T(8,128)S(1)} %get-tuple-element.21.mid.refs_2_, f32[3,32,128]{2,1,0:T(8,128)S(1)} %get-tuple-element.24.line.refs_3_, ...), custom_call_target="tpu_custom_call" | custom-call | flops 3000000000 | tf_op jit(solution)/shard_map/moments/pallas_call | solution.py:361
  18.1 0.0 collective-permute-done.1.refs_8_
  18.1 0.0 collective-permute-done.2.refs_9_
  18.1 22.3 %pairs.1 = (f32[3,8,896]{2,1,0:T(8,128)S(1)}, f32[3,8,896]{2,1,0:T(8,128)S(1)}) custom-call(s32[400]{0:T(512)S(1)} %get-tuple-element.22.refs_0_, f32[32,3,128,128]{3,2,1,0:T(8,128)S(1)} %get-tuple-element.23.refs_1_, f32[3,32,128]{2,1,0:T(8,128)S(1)} %get-tuple-element.21.mid.refs_2_, f32[3,32,128]{2,1,0:T(8,128)S(1)} %get-tuple-element.24.line.refs_3_, ...), custom_call_target="tpu_custom_call" | custom-call | flops 10000000000 | tf_op jit(solution)/shard_map/pairs/pallas_call | solution.py:384
  40.5 0.1 collective-permute-start.3
  40.5 4.5 %collective-permute-done.3 = f32[3,8,896]{2,1,0:T(8,128)S(1)} collective-permute-done((f32[3,8,896]{2,1,0:T(8,128)S(1)}, f32[3,8,896]{2,1,0:T(8,128)S(1)}, u32[]{:S(2)}, u32[]{:S(2)}) %collective-permute-start.3) | collective-permute-done | bytes 86048 | tf_op jit(solution)/shard_map/ppermute | solution.py:29
  45.1 1.9 %collective-permute-start.5 = (f32[8,896]{1,0:T(8,128)S(1)}, f32[8,896]{1,0:T(8,128)S(1)}, u32[]{:S(2)}, u32[]{:S(2)}) collective-permute-start(f32[8,896]{1,0:T(8,128)S(1)} %get-tuple-element.40), channel_id=1, source_target_pairs={{1,0},{2,1},{3,2},{4,3},{5,4},{6,5},{7,6},{8,7},{9,8},{10,9},{11,1... | collective-permute-start | bytes 86024 | tf_op jit(solution)/shard_map/ppermute | solution.py:29
  47.0 0.0 collective-permute-start.4
  47.0 1.6 %collective-permute-done.5.second = f32[8,896]{1,0:T(8,128)S(1)} collective-permute-done((f32[8,896]{1,0:T(8,128)S(1)}, f32[8,896]{1,0:T(8,128)S(1)}, u32[]{:S(2)}, u32[]{:S(2)}) %collective-permute-start.5) | collective-permute-done | bytes 28704 | tf_op jit(solution)/shard_map/ppermute | solution.py:29
  48.5 4.4 %collective-permute-done.4.first = f32[8,896]{1,0:T(8,128)S(1)} collective-permute-done((f32[8,896]{1,0:T(8,128)S(1)}, f32[8,896]{1,0:T(8,128)S(1)}, u32[]{:S(2)}, u32[]{:S(2)}) %collective-permute-start.4) | collective-permute-done | bytes 28704 | tf_op jit(solution)/shard_map/ppermute | solution.py:29
  53.0 0.6 %finish.1 = (f32[3,4,128]{2,1,0:T(4,128)}, f32[8,315]{1,0:T(8,128)}) custom-call(f32[3,8,896]{2,1,0:T(8,128)S(1)} %add.3.middle, f32[8,896]{1,0:T(8,128)S(1)} %collective-permute-done.4.first, f32[8,896]{1,0:T(8,128)S(1)} %collective-permute-done.5.second), custom_call_target="tpu_custom_call" | custom-call | tf_op jit(solution)/shard_map/finish/pallas_call | solution.py:404
  (5 shorter events, 0.0 us)
Async XLA Ops:
  1.8 8.3 %collective-permute-start = (f32[12,8,128]{2,1,0:T(8,128)S(1)}, f32[12,8,128]{2,1,0:T(8,128)S(1)}, u32[]{:S(2)}, u32[]{:S(2)}) collective-permute-start(f32[12,8,128]{2,1,0:T(8,128)S(1)} %get-tuple-element.29), channel_id=1, source_target_pairs={{16,0},{0,16},{17,1},{1,17},{18,2},{2,18},{19,3},{3,19},{20,4},{4,... | collective-permute-start | bytes 147464 | tf_op jit(solution)/shard_map/ppermute | solution.py:29
  10.1 8.0 %collective-permute-start.1 = (f32[6,8,128]{2,1,0:T(8,128)S(1)}, f32[6,8,128]{2,1,0:T(8,128)S(1)}, u32[]{:S(2)}, u32[]{:S(2)}) collective-permute-start(f32[6,8,128]{2,1,0:T(8,128)S(1)} %pad_maximum_fusion), channel_id=1, source_target_pairs={{15,0},{0,1},{1,2},{2,3},{3,4},{4,5},{5,6},{6,7},{7,8},{8,9},{9,10... | collective-permute-start | bytes 73736 | tf_op jit(solution)/shard_map/ppermute | solution.py:29
  10.2 8.0 %collective-permute-start.2 = (f32[6,8,128]{2,1,0:T(8,128)S(1)}, f32[6,8,128]{2,1,0:T(8,128)S(1)}, u32[]{:S(2)}, u32[]{:S(2)}) collective-permute-start(f32[6,8,128]{2,1,0:T(8,128)S(1)} %pad_maximum_fusion.1), channel_id=1, source_target_pairs={{1,0},{2,1},{3,2},{4,3},{5,4},{6,5},{7,6},{8,7},{9,8},{10,9},{11,1... | collective-permute-start | bytes 73736 | tf_op jit(solution)/shard_map/ppermute | solution.py:29
  40.5 4.6 %collective-permute-start.3 = (f32[3,8,896]{2,1,0:T(8,128)S(1)}, f32[3,8,896]{2,1,0:T(8,128)S(1)}, u32[]{:S(2)}, u32[]{:S(2)}) collective-permute-start(f32[3,8,896]{2,1,0:T(8,128)S(1)} %get-tuple-element.33), channel_id=1, source_target_pairs={{16,0},{0,16},{17,1},{1,17},{18,2},{2,18},{19,3},{3,19},{20,4},{4,... | collective-permute-start | bytes 258056 | tf_op jit(solution)/shard_map/ppermute | solution.py:29
  45.1 3.5 %collective-permute-start.5 = (f32[8,896]{1,0:T(8,128)S(1)}, f32[8,896]{1,0:T(8,128)S(1)}, u32[]{:S(2)}, u32[]{:S(2)}) collective-permute-start(f32[8,896]{1,0:T(8,128)S(1)} %get-tuple-element.40), channel_id=1, source_target_pairs={{1,0},{2,1},{3,2},{4,3},{5,4},{6,5},{7,6},{8,7},{9,8},{10,9},{11,1... | collective-permute-start | bytes 86024 | tf_op jit(solution)/shard_map/ppermute | solution.py:29
  47.0 6.0 %collective-permute-start.4 = (f32[8,896]{1,0:T(8,128)S(1)}, f32[8,896]{1,0:T(8,128)S(1)}, u32[]{:S(2)}, u32[]{:S(2)}) collective-permute-start(f32[8,896]{1,0:T(8,128)S(1)} %get-tuple-element.41), channel_id=1, source_target_pairs={{15,0},{0,1},{1,2},{2,3},{3,4},{4,5},{5,6},{6,7},{7,8},{8,9},{9,10... | collective-permute-start | bytes 86024 | tf_op jit(solution)/shard_map/ppermute | solution.py:29
